TPU v7x, 32 devices: a whole 2x2x4 slice. The times are simulated.
32 devices in a mesh: ens: 2 (over x), lat: 16 (over z, y, core).
Axes of the slice: x: 2, y: 2, z: 4, core: 2. Of those that a mesh axis runs over, the one named last changes fastest.
Arguments:
- members: float32 [80, 2, 64, 640], P('lat', 'ens'), may hold values from -24 to 24
- truth: float32 [4, 80, 64, 640], P(None, 'lat'), may hold values from -32 to 32
- target_time: int32 [80], P('lat'), may hold values from 0 to 3
- row_taps: int32 [1, 80, 5], P(None, 'lat'), may hold values from 0 to 79, as said below
- filters: float32 [1, 80, 5, 9, 5], P(None, 'lat'), may hold values from -1.2 to 1.2
- mixing: float32 [1, 64, 9, 64], replicated, may hold values from -0.25 to 0.25
Outputs:
- score_grad: float32 [80, 2, 64, 640], P('lat', 'ens')
- loss_value: float32 [1], replicated
Inputs may be any that keep to these rules, and one draw needn't show every extreme that they name: row_taps[l, i, t] lies within 4 rows of i; in every layer some row lists a row exactly 4 below it and some row one exactly 4 above it. `target_time`: selects one of the stored target fields for each latitude row.
All inputs are finite; a program needn't handle non-finite values.
Results may differ from a plain program's by a relative error of at most 0.0003.
Values sent between devices are 32-bit elements; how exact they have to be, the bound alone decides.
No kernel may reach another device: no remote copies, remote signals or barrier semaphores. Data moves between devices by JAX's collectives and lax.ppermute only.
A program may use at most 64 MiB of HBM per device.

v0:
```python
import math

import jax
import jax.numpy as jnp
from jax import lax
from jax.sharding import PartitionSpec as P

C = 64
NLON = 640
K = 9
LW = 5
REACH = 4


def padded(cells, sides, width):
    for axis, dim in sides:
        count = lax.axis_size(axis)
        ends = count - 1
        head = lax.slice_in_dim(cells, 0, width, axis=dim)
        tail = lax.slice_in_dim(cells, cells.shape[dim] - width, cells.shape[dim], axis=dim)
        cells = jnp.concatenate(
            [
                lax.ppermute(tail, axis, [(i, (i + 1) % count) for i in range(ends)]),
                cells,
                lax.ppermute(head, axis, [((i + 1) % count, i) for i in range(ends)]),
            ],
            axis=dim,
        )
    return cells


def area_weights(total_rows, first_row, band_rows):
    latitude = (jnp.arange(total_rows, dtype=jnp.float32) + 0.5) * (
        math.pi / total_rows
    ) - 0.5 * math.pi
    cosine = jnp.cos(latitude)
    return lax.dynamic_slice_in_dim(cosine / jnp.mean(cosine), first_row, band_rows)


def score_cells(grouped, target_piece, area):
    total_members = grouped.shape[1]
    to_truth = grouped - target_piece[:, None]
    skill_dist = jnp.sqrt(jnp.mean(to_truth * to_truth, axis=2) + 1.0)

    def pair_terms(member):
        gap_field = member[:, None] - grouped
        distance = jnp.sqrt(jnp.mean(gap_field * gap_field, axis=2) + 1.0)
        return (jnp.sum(gap_field / distance[:, :, None], axis=1), jnp.sum(distance, axis=1))

    pull_sum, spread = lax.map(pair_terms, jnp.moveaxis(grouped, 1, 0))
    grad_piece = area[:, None, None, None] * (
        to_truth / skill_dist[:, :, None] - jnp.moveaxis(pull_sum, 0, 1) / total_members
    )
    per_cell = jnp.sum(skill_dist, axis=1) / total_members - jnp.sum(spread, axis=0) / (
        2.0 * total_members * total_members
    )
    return (grad_piece, jnp.sum(area[:, None] * per_cell))


def per_device(members, truth, target_time, row_taps, filters, mixing):
    highest = lax.Precision.HIGHEST
    band_rows = members.shape[0]
    own_count = members.shape[1]
    lon_cells = members.shape[3]
    half_width = LW // 2
    first_row = lax.axis_index("lat") * band_rows
    total_rows = band_rows * lax.axis_size("lat")
    extended_rows = band_rows + 2 * REACH
    fields = members
    extended = padded(fields, (("lat", 0),), REACH)
    local_taps = row_taps[0] - (first_row - REACH)
    one_hot = (
        local_taps[:, :, None] == jnp.arange(extended_rows, dtype=jnp.int32)[None, None, :]
    ).astype(jnp.float32)
    coupling = jnp.einsum("rtkd,rtq->rkdq", filters[0], one_hot, precision=highest)
    shifted = jnp.stack(
        [jnp.roll(extended, half_width - lon_lag, axis=3) for lon_lag in range(LW)], axis=0
    )
    basis_out = jnp.dot(
        coupling.reshape(band_rows * K, LW * extended_rows),
        shifted.reshape(LW * extended_rows, -1),
        precision=highest,
        preferred_element_type=jnp.float32,
    )
    basis_out = basis_out.reshape(band_rows, K, own_count, C, lon_cells)
    mixed_out = jnp.einsum("okc,rkmcj->rmoj", mixing[0], basis_out, precision=highest)
    fields = fields + jax.nn.gelu(mixed_out, approximate=True)
    stored_count = truth.shape[0]
    selector = (target_time[None, :] == jnp.arange(stored_count, dtype=jnp.int32)[:, None]).astype(
        jnp.float32
    )
    target = jnp.sum(selector[:, :, None, None] * truth, axis=0)
    area = area_weights(total_rows, first_row, band_rows)
    piece_width = lon_cells // lax.axis_size("ens")
    grouped = lax.all_to_all(fields, "ens", split_axis=3, concat_axis=1, tiled=True)
    target_piece = lax.dynamic_slice_in_dim(
        target, lax.axis_index("ens") * piece_width, piece_width, 2
    )
    grad_piece, loss_part = score_cells(grouped, target_piece, area)
    score_grad = lax.all_to_all(grad_piece, "ens", split_axis=1, concat_axis=3, tiled=True)
    loss_value = lax.psum(jnp.reshape(loss_part, (1,)), ("ens", "lat")) / (total_rows * NLON)
    return (score_grad, loss_value)


def solution(mesh):
    placed = (
        P("lat", "ens", None, None),
        P(None, "lat", None, None),
        P("lat"),
        P(None, "lat", None),
        P(None, "lat", None, None, None),
        P(),
    )
    return jax.shard_map(
        per_device,
        mesh=mesh,
        in_specs=placed,
        out_specs=(P("lat", "ens", None, None), P()),
        check_vma=False,
    )
```

profile of v0, /device:TPU:0, one launch (start us, length us, event | category | flops | bytes accessed | tf_op | source)
XLA Modules:
  0.0 150.1 jit_solution(9014483626603416416)
XLA Ops:
  0.6 0.0 copy-start
  0.6 0.0 copy-start.2
  0.7 0.0 copy-start.7
  0.7 0.0 copy-start.6
  0.7 0.0 copy-start.8
  0.7 1.5 fusion.38
  2.2 3.2 %collective-permute-start = (f32[4,1,64,640]{3,2,1,0:T(8,128)S(1)}, f32[4,1,64,640]{3,2,1,0:T(8,128)}, u32[]{:S(2)}, u32[]{:S(2)}) collective-permute-start(f32[4,1,64,640]{3,2,1,0:T(8,128)S(1)} %get-tuple-element.107), channel_id=1, source_target_pairs={{0,1},{1,2},{2,3},{3,4},{4,5},{5,6},{6,7},{7,8},{8,9},{9,10},{10,1... | collective-permute-start | bytes 1966088 | tf_op jit(solution)/shard_map/ppermute | solution.py:23
  5.4 1.3 collective-permute-start.1
  6.7 0.0 copy-done.7
  6.7 0.4 convolution_bitcast_fusion
  7.1 0.1 copy.175
  7.3 0.7 fusion.34
  8.6 0.0 collective-permute-done
  8.6 1.1 constant_dynamic-update-slice_fusion.2
  9.8 0.1 constant_dynamic-update-slice_fusion.1
  9.8 0.8 collective-permute-done.1
  10.7 0.2 slice.48
  10.9 0.7 fusion.36
  11.6 0.2 fusion.37
  11.8 0.6 slice.54
  12.5 0.6 fusion.6
  13.1 0.6 fusion.7
  13.7 0.2 bitcast_dynamic-update-slice_fusion.2
  13.9 0.3 fusion.8
  14.2 0.3 fusion.9
  14.5 4.7 %slice_bitcast_fusion = f32[64,640,65]{1,0,2:T(8,128)} fusion(f32[65,64,640]{2,1,0:T(8,128)S(1)} %bitcast.123), kind=kLoop, calls=%fused_computation.10 | loop fusion | bytes 21299200 | tf_op jit(solution)/shard_map/reshape.23
  19.2 23.5 %fusion.1 = f32[5,9,64,640]{3,0,2,1:T(8,128)S(1)} fusion(f32[5,9,65,1]{2,0,3,1:T(8,128)S(1)} %copy.175, f32[64,640,65]{1,0,2:T(8,128)} %slice_bitcast_fusion), kind=kOutput, calls=%fused_computation.7 | convolution fusion | flops 1437696000 | bytes 18034100 | tf_op jit(solution)/shard_map/dot_general | solution.py:79
  42.7 5.5 %fusion.23 = f32[5,1,64,640]{3,2,0,1:T(8,128)S(1)} fusion(f32[5,9,64,640]{3,0,2,1:T(8,128)S(1)} %fusion.1, f32[5,1,64,640]{3,2,1,0:T(8,128)S(1)} %copy-done.2, f32[1,64,9,64]{3,1,2,0:T(8,128)S(1)} %copy-done), kind=kOutput, calls=%fused_computation.39 | convolution fusion | flops 1417420800 | bytes 9158656 | tf_op jit(solution)/shard_map/okc,rkmcj->rmoj/dot_general | solution.py:86
  48.2 2.8 %copy.168 = f32[5,1,64,640]{2,1,0,3:T(1,128)} copy(f32[5,1,64,640]{3,2,0,1:T(8,128)S(1)} %fusion.23) | data formatting | bytes 1638400 | tf_op jit(solution)/shard_map/add | solution.py:87
  51.0 0.5 broadcast.77
  51.4 6.1 %reduce = f32[640,5,64]{2,1,0:T(8,128)S(1)} reduce(f32[640,5,1,64]{3,2,1,0:T(1,128)} %bitcast.125, f32[]{:T(128)} %broadcast.77), dimensions={2}, to_apply=%bitcast.106.reduce_sub_computation | reduce | bytes 1638404
  57.5 1.9 %reshape.73 = f32[2,1,102400]{2,1,0:T(1,128)} reshape(f32[640,5,64]{2,1,0:T(8,128)S(1)} %reduce) | data formatting | bytes 1638400
  59.5 3.8 %all-to-all-start = ((f32[2,1,102400]{2,1,0:T(1,128)}), f32[2,1,102400]{2,1,0:T(1,128)S(1)}, u32[]{:S(2)}, u32[]{:S(2)}) async-start(f32[2,1,102400]{2,1,0:T(1,128)} %reshape.73), calls=%async_computation | async-start | bytes 1638400 | tf_op jit(solution)/shard_map/all_to_all | solution.py:95
  63.3 0.1 broadcast_divide_fusion
  63.4 0.1 dynamic_slice.10
  63.4 2.4 %multiply_reduce_fusion.1 = f32[5,64,640]{2,1,0:T(8,128)S(1)} fusion(f32[4,5,64,640]{3,2,1,0:T(8,128)} %param.9, f32[4,5]{1,0:T(4,128)S(1)} %fusion.33), kind=kLoop, calls=%fused_computation.13 | loop fusion | flops 1433600 | bytes 4096080 | tf_op jit(solution)/shard_map/reduce_sum | solution.py:92
  65.8 1.0 constant_dynamic-slice_fusion
  66.8 4.4 %all-to-all-done = f32[2,1,102400]{2,1,0:T(1,128)S(1)} async-done(((f32[2,1,102400]{2,1,0:T(1,128)}), f32[2,1,102400]{2,1,0:T(1,128)S(1)}, u32[]{:S(2)}, u32[]{:S(2)}) %all-to-all-start) | async-done | bytes 819232 | tf_op jit(solution)/shard_map/all_to_all | solution.py:95
  71.2 3.1 %reduce.1 = f32[2,102400]{1,0:T(2,128)S(1)} reduce(f32[2,1,102400]{2,1,0:T(1,128)S(1)} %all-to-all-done, f32[]{:T(128)} %broadcast.77), dimensions={1}, to_apply=%all_to_all.26.reduce_sub_computation | reduce | bytes 1638404 | tf_op jit(solution)/shard_map/all_to_all | solution.py:95
  74.3 2.2 %reshape.74 = f32[640,5,1,64]{3,2,1,0:T(1,128)S(1)} reshape(f32[2,102400]{1,0:T(2,128)S(1)} %reduce.1) | data formatting | bytes 1638400
  76.5 1.9 %copy.169 = f32[5,1,64,640]{3,2,0,1:T(8,128)S(1)} copy(f32[5,1,64,640]{2,1,0,3:T(1,128)S(1)} %bitcast.126) | data formatting | bytes 1638400 | tf_op jit(solution)/shard_map/all_to_all | solution.py:95
  78.4 0.7 all_to_all.27
  79.2 0.1 copy.207
  79.3 0.1 copy.208
  79.4 4.4 %while.12 = (s32[]{:T(128)}, f32[2,5,64,320]{3,2,1,0:T(8,128)}, f32[2,5,320]{2,1,0:T(8,128)S(1)}, f32[2,5,64,320]{3,2,1,0:T(8,128)S(1)}, f32[5,2,64,320]{3,2,1,0:T(8,128)S(1)}, /*index=5*/s32[]{:T(128)}) while((s32[]{:T(128)}, f32[2,5,64,320]{3,2,1,0:T(8,128)}, f32[2,5,320]{2,1,0:T(8,128)S(1)}, f32[2,5,64,320]{3,2,1,0:T(8,128)S(1)}, ...), condition=%wide.region_7.8_spmd, body=%wide.region_3.7_spmd.sunk | while | flops 1131202 | bytes 11305353 | solution.py:50
  79.4 0.2 multiply_reduce_fusion.5
  79.6 0.1 divide_reduce_fusion.2
  79.8 0.8 copy-done.3
  80.6 0.0 copy-start.4
  80.6 0.9 copy-done.4
  81.6 0.2 multiply_reduce_fusion.5
  81.8 0.1 divide_reduce_fusion.2
  82.0 0.8 copy-done.3
  82.8 0.9 copy-done.4
  83.8 1.3 multiply_reduce_fusion.2
  85.1 0.1 copy-done.5
  85.1 2.2 %fusion.13 = f32[5,2,64,320]{3,2,0,1:T(8,128)} fusion(f32[2,5,64,320]{3,2,1,0:T(8,128)S(1)} %copy-done.5, f32[5,1,64,2,320]{4,3,2,0,1:T(2,128)S(1)} %all_to_all.27, f32[5,2,320]{2,0,1:T(8,128)S(1)} %get-tuple-element.109, f32[5,64,320]{2,1,0:T(8,128)} %constant_dynamic-slice_fusion, f32[5]{0:T(128)S(1)} %dynamic_slice.10), kind=kLoop, calls=%fused_computation.27 | loop fusion | flops 1024000 | bytes 2880020 | tf_op jit(solution)/shard_map/mul | solution.py:51
  87.4 3.6 %all-to-all-start.1 = ((f32[5,2,64,320]{3,2,0,1:T(8,128)}), f32[5,2,64,320]{3,2,0,1:T(8,128)S(1)}, u32[]{:S(2)}, u32[]{:S(2)}) async-start(f32[5,2,64,320]{3,2,0,1:T(8,128)} %fusion.13), calls=%async_computation.1 | async-start | bytes 1966080 | tf_op jit(solution)/shard_map/all_to_all | solution.py:100
  90.9 0.0 copy-start.1
  91.0 0.7 multiply_reduce_fusion.3
  91.6 54.3 %psum.7 = f32[1]{0:T(128)} all-reduce(f32[1]{0:T(128)} %bitcast.39), channel_id=1, replica_groups=mesh['ens'=2,'lat'=16] {'ens','lat'}, use_global_device_ids=true, to_apply=%region_11.12 | all-reduce | flops 1 | bytes 8 | tf_op jit(solution)/shard_map/psum | solution.py:101
  146.6 0.0 all-to-all-done.1
  146.7 0.8 copy.172
  147.4 1.6 %all_to_all.33 = f32[5,1,64,640]{3,2,0,1:T(8,128)} reshape(f32[5,1,64,2,320]{4,3,2,0,1:T(2,128)S(1)} %copy.172) | data formatting | bytes 1638400 | tf_op jit(solution)/shard_map/all_to_all | solution.py:100
  (26 shorter events, 0.4 us)
Async XLA Ops:
  0.6 42.1 %copy-start = (f32[1,64,9,64]{3,1,2,0:T(8,128)S(1)}, f32[1,64,9,64]{3,1,2,0:T(8,128)}, u32[]{:S(2)}) copy-start(f32[1,64,9,64]{3,1,2,0:T(8,128)} %param.13) | copy-start | bytes 442372
  0.6 9.1 %copy-start.2 = (f32[5,1,64,640]{3,2,1,0:T(8,128)S(1)}, f32[5,1,64,640]{3,2,1,0:T(8,128)}, u32[]{:S(2)}) copy-start(f32[5,1,64,640]{3,2,1,0:T(8,128)} %param.8) | copy-start | bytes 2457604
  0.7 6.0 %copy-start.7 = (s32[1,5,5]{2,0,1:T(1,128)S(1)}, s32[1,5,5]{2,0,1:T(1,128)}, u32[]{:S(2)}) copy-start(s32[1,5,5]{2,0,1:T(1,128)} %param.11) | copy-start | bytes 304
  0.7 6.0 %copy-start.6 = (f32[1,5,5,9,5]{3,0,4,2,1:T(1,128)S(1)}, f32[1,5,5,9,5]{3,0,4,2,1:T(1,128)}, u32[]{:S(2)}) copy-start(f32[1,5,5,9,5]{3,0,4,2,1:T(1,128)} %param.12) | copy-start | bytes 13504
  0.7 7.9 %copy-start.8 = (s32[5]{0:T(128)S(1)}, s32[5]{0:T(128)}, u32[]{:S(2)}) copy-start(s32[5]{0:T(128)} %param.10) | copy-start | bytes 64
  2.2 6.5 %collective-permute-start = (f32[4,1,64,640]{3,2,1,0:T(8,128)S(1)}, f32[4,1,64,640]{3,2,1,0:T(8,128)}, u32[]{:S(2)}, u32[]{:S(2)}) collective-permute-start(f32[4,1,64,640]{3,2,1,0:T(8,128)S(1)} %get-tuple-element.107), channel_id=1, source_target_pairs={{0,1},{1,2},{2,3},{3,4},{4,5},{5,6},{6,7},{7,8},{8,9},{9,10},{10,1... | collective-permute-start | bytes 1966088 | tf_op jit(solution)/shard_map/ppermute | solution.py:23
  5.4 5.3 %collective-permute-start.1 = (f32[4,1,64,640]{3,2,1,0:T(8,128)S(1)}, f32[4,1,64,640]{3,2,1,0:T(8,128)S(1)}, u32[]{:S(2)}, u32[]{:S(2)}) collective-permute-start(f32[4,1,64,640]{3,2,1,0:T(8,128)S(1)} %get-tuple-element.106), channel_id=1, source_target_pairs={{1,0},{2,1},{3,2},{4,3},{5,4},{6,5},{7,6},{8,7},{9,8},{10,9},{11,1... | collective-permute-start | bytes 1966088 | tf_op jit(solution)/shard_map/ppermute | solution.py:25
  59.5 11.7 %all-to-all-start = ((f32[2,1,102400]{2,1,0:T(1,128)}), f32[2,1,102400]{2,1,0:T(1,128)S(1)}, u32[]{:S(2)}, u32[]{:S(2)}) async-start(f32[2,1,102400]{2,1,0:T(1,128)} %reshape.73), calls=%async_computation | async-start | bytes 1638400 | tf_op jit(solution)/shard_map/all_to_all | solution.py:95
  79.4 1.2 copy-start.3
  80.6 1.0 copy-start.4
  81.6 1.2 copy-start.3
  82.8 1.0 copy-start.4
  83.8 1.3 copy-start.5
  87.4 59.3 %all-to-all-start.1 = ((f32[5,2,64,320]{3,2,0,1:T(8,128)}), f32[5,2,64,320]{3,2,0,1:T(8,128)S(1)}, u32[]{:S(2)}, u32[]{:S(2)}) async-start(f32[5,2,64,320]{3,2,0,1:T(8,128)} %fusion.13), calls=%async_computation.1 | async-start | bytes 1966080 | tf_op jit(solution)/shard_map/all_to_all | solution.py:100
  90.9 58.0 %copy-start.1 = (f32[1,64,9,64]{3,1,2,0:T(8,128)S(1)}, f32[1,64,9,64]{3,1,2,0:T(8,128)}, u32[]{:S(2)}) copy-start(f32[1,64,9,64]{3,1,2,0:T(8,128)} %param.13) | copy-start | bytes 442372
where the time goes:
time: 151 us; the launch traced here: 150 us
  blocking collectives  54.3 us (36%)
  matrix products  29.4 us (19%)
  local copies, waits for them, and re-layouts  26.8 us (18%)
  other arithmetic  19 us (13%)
  starting transfers between devices  11.9 us (8%)
  waiting for transfers between devices  5.19 us (3%)
  between operations  3.43 us (2%)
    psum x1, blocking collectives, per_device(): lax.psum(jnp.reshape(loss_part, (1,)), ('ens', 'lat')) / (total_rows * NLON)  54.3 us
    dot_general x1, matrix products, per_device(): jnp.dot(coupling.reshape(band_rows * K, LW * extended_rows), shifted.resh...  23.5 us
    unnamed x4, other arithmetic  7.63 us
    unnamed x20, local copies, waits for them, and re-layouts  6.1 us
    dot_general x1, matrix products, per_device(): jnp.einsum('okc,rkmcj->rmoj', mixing[0], basis_out, precision=highest)  5.48 us
    another operation x1, local copies, waits for them, and re-layouts  4.71 us
    all_to_all x1, waiting for transfers between devices, per_device(): lax.all_to_all(fields, 'ens', split_axis=3, concat_axis=1, tiled=True)  4.35 us
    all_to_all x1, starting transfers between devices, per_device(): lax.all_to_all(fields, 'ens', split_axis=3, concat_axis=1, tiled=True)  3.8 us
  transfers between devices with their start and end apart: 4, of which 2 were waited for; matrix products, arithmetic and copies ran while one was open for 4% of the time, Pallas kernels for 0%

commit v1 on v0

v1 whole, which is shorter than its diff:
```python
import functools
import math

import jax
import jax.numpy as jnp
import numpy as np
from jax import lax
from jax.experimental import pallas as pl
from jax.experimental.pallas import tpu as pltpu
from jax.sharding import PartitionSpec as P

REACH = 4
LANES = 128
GROUP = 8
MIB = 1 << 20

VMEM = pl.BlockSpec(memory_space=pltpu.VMEM)
SMEM = pl.BlockSpec(memory_space=pltpu.SMEM)
ANY = pl.BlockSpec(memory_space=pl.ANY)


def round_up(value, unit):
    return -(-value // unit) * unit


def shift_left(cells, amount):
    width = cells.shape[-1]
    amount %= width
    return cells if amount == 0 else pltpu.roll(cells, width - amount, axis=cells.ndim - 1)


def pack_rows(ref, at, cells, width):
    groups = cells.shape[0] // GROUP
    lane = lax.broadcasted_iota(jnp.int32, (GROUP, LANES), 1)
    held = None
    for group in range(groups):
        part = cells[group * GROUP : (group + 1) * GROUP]
        first, last = group * width, (group + 1) * width
        offset = first % LANES
        tiles = -(-(offset + width) // LANES)
        pad = tiles * LANES - part.shape[1]
        if pad > 0:
            part = jnp.concatenate([part, jnp.zeros((GROUP, pad), part.dtype)], axis=1)
        if offset:
            part = pltpu.roll(part, offset, axis=1)
        base = first // LANES
        for tile in range(tiles):
            value = part[:, tile * LANES : (tile + 1) * LANES]
            if tile == 0 and offset:
                value = jnp.where(lane < offset, held, value)
            if (base + tile + 1) * LANES <= last or group == groups - 1:
                ref[at + (slice(None), pl.ds((base + tile) * LANES, LANES))] = value
            else:
                held = value


def unpack_rows(ref, at, groups, width, wide):
    parts = []
    limit = ref.shape[-1]
    for group in range(groups):
        first = group * width
        offset = first % LANES
        base = first - offset
        take = min(wide + (LANES if offset else 0), limit - base)
        part = ref[at + (slice(None), pl.ds(base, take))]
        if take < wide:
            part = jnp.concatenate([part, jnp.zeros((GROUP, wide - take), part.dtype)], axis=1)
        if offset:
            part = shift_left(part, offset)
        parts.append(part[:, :wide])
    return jnp.concatenate(parts, axis=0)


def gelu(v):
    return 0.5 * v * (1.0 + jnp.tanh(math.sqrt(2.0 / math.pi) * (v + 0.044715 * (v * v * v))))


def prepare_kernel(sizes, members, own_w, near_own, far_own, oth, far_oth):
    band, n, w, reach2, wide = sizes
    ens = lax.axis_index("ens")
    odd = lax.rem(lax.axis_index("lat"), 2)
    total = members.shape[3]
    kept = w + 2 * reach2

    def one_row(r, _):
        row = members[r, 0]

        def window(owner):
            start = lax.rem(owner * w - reach2 + total, total)
            return pltpu.roll(row, lax.rem(total - start, total), axis=1)[:, :wide]

        own = window(ens)
        own_w[r] = own

        near_at = r - (1 - odd)
        far_at = r - odd
        keep_near = jnp.logical_and(near_at >= 0, near_at < REACH)
        keep_far = jnp.logical_and(far_at >= 0, far_at < REACH)

        @pl.when(keep_near)
        def _():
            pack_rows(near_own, (near_at,), own, kept)

        @pl.when(keep_far)
        def _():
            pack_rows(far_own, (far_at,), own, kept)

        for step in range(1, n):
            cells = window(lax.rem(ens + step, n))
            pack_rows(oth, (step - 1, r), cells, kept)

            @pl.when(keep_far)
            def _():
                far_oth[step - 1, far_at] = oth[step - 1, r]

        return 0

    lax.fori_loop(0, band, one_row, 0)


def weights_kernel(sizes, times, filters, mix, truth, weights, target, held, sems):
    band, taps, lags, kinds, w, wide = sizes
    ens = lax.axis_index("ens")
    total = truth.shape[3]
    copies = [
        pltpu.make_async_copy(truth.at[times[r], r], held.at[r], sems.at[r]) for r in range(band)
    ]
    for copy in copies:
        copy.start()
    c = mix.shape[1]
    half = lax.broadcasted_iota(jnp.int32, (c, 2 * c), 1) < c

    def one_row(r, _):
        for d in range(lags):
            rows = pl.ds(d * c, c)
            before = None
            for t in range(taps):
                acc = filters[r * taps + t, d] * mix[0]
                for k in range(1, kinds):
                    acc = acc + filters[r * taps + t, k * lags + d] * mix[k]
                high = acc.astype(jnp.bfloat16).astype(jnp.float32)
                low = acc - high
                weights[r, rows, pl.ds(t * 2 * c, 2 * c)] = jnp.where(half, high, low).astype(
                    jnp.bfloat16
                )
                if t % 2:
                    pair = jnp.where(half, before, high)
                elif t == taps - 1:
                    pair = jnp.where(half, high, 0.0)
                if t % 2 or t == taps - 1:
                    weights[r, rows, pl.ds((taps + t // 2) * 2 * c, 2 * c)] = pair.astype(jnp.bfloat16)
                before = high
        return 0

    lax.fori_loop(0, band, one_row, 0)
    for copy in copies:
        copy.wait()

    def cut(r, _):
        turn = lax.rem(total - ens * w, total)
        target[r] = pltpu.roll(held[r], turn, axis=1)[:, :wide]
        return 0

    lax.fori_loop(0, band, cut, 0)


def store_split(split, q, cells):
    c = cells.shape[0]
    high = cells.astype(jnp.bfloat16)
    split[q, pl.ds(0, c)] = high
    split[q, pl.ds(c, c)] = (cells - high.astype(jnp.float32)).astype(jnp.bfloat16)


def store_halo(split, near, near_at, far, far_at, kept, wide, band):
    odd = lax.rem(lax.axis_index("lat"), 2)
    groups = split.shape[1] // 2 // GROUP
    low_base = REACH + band

    def one(i, _):
        store_split(split, i + low_base * (1 - odd), unpack_rows(near, near_at + (i,), groups, kept, wide))
        store_split(split, i + low_base * odd, unpack_rows(far, far_at + (i,), groups, kept, wide))
        return 0

    lax.fori_loop(0, REACH, one, 0)


def convolve(row_taps, weights, split, stack, r, lags):
    c = split.shape[1] // 2
    taps = row_taps.shape[1]
    for t in range(taps):
        q = row_taps[r, t]
        high = split[q, pl.ds(0, c)]
        stack[pl.ds(2 * t * c, c)] = high
        stack[pl.ds((2 * t + 1) * c, c)] = high
        stack[pl.ds((2 * taps + t) * c, c)] = split[q, pl.ds(c, c)]
    products = jnp.dot(weights[r], stack[...], preferred_element_type=jnp.float32)
    mixed = products[0:c]
    for d in range(1, lags):
        mixed = mixed + shift_left(products[d * c : (d + 1) * c], d)
    return mixed


def clear_tail(stack, taps, c):
    if stack.shape[0] > 3 * taps * c:
        rest = stack.shape[0] - 3 * taps * c
        stack[pl.ds(3 * taps * c, rest)] = jnp.zeros((rest, stack.shape[1]), stack.dtype)


def own_kernel(sizes, row_taps, weights, own_w, near, far, x_own, split, stack):
    band, lags, w, reach2, wide = sizes
    kept = w + 2 * reach2
    clear_tail(stack, row_taps.shape[1], own_w.shape[1])
    store_halo(split, near, (), far, (), kept, wide, band)

    def own(r, _):
        store_split(split, REACH + r, own_w[r])
        return 0

    lax.fori_loop(0, band, own, 0)

    def one_row(r, _):
        mixed = convolve(row_taps, weights, split, stack, r, lags)
        x_own[r] = shift_left(own_w[r], reach2) + gelu(mixed)
        return 0

    lax.fori_loop(0, band, one_row, 0)


def score_kernel(
    sizes, row_taps, area, weights, x_own, oth, near, far, target, g_own, g_oth, loss, split, stack, states
):
    band, n, lags, w, reach2, wide = sizes
    kept = w + 2 * reach2
    c = x_own.shape[1]
    groups = c // GROUP
    clear_tail(stack, row_taps.shape[1], c)
    for step in range(n - 1):
        store_halo(split, near, (step,), far, (step,), kept, wide, band)

        def own(r, _):
            cells = unpack_rows(oth, (step, r), groups, kept, wide)
            store_split(split, REACH + r, cells)
            states[step, r] = shift_left(cells, reach2)
            return 0

        lax.fori_loop(0, band, own, 0)

        def one_row(r, _):
            mixed = convolve(row_taps, weights, split, stack, r, lags)
            states[step, r] = states[step, r] + gelu(mixed)
            return 0

        lax.fori_loop(0, band, one_row, 0)

    def score(r, total):
        weight = area[r]
        truth = target[r]
        xs = [x_own[r]] + [states[step, r] for step in range(n - 1)]
        mean = 1.0 / c
        cell = None
        grads = []
        for x in xs:
            gap = x - truth
            skill = jnp.sqrt(jnp.sum(gap * gap, axis=0, keepdims=True) * mean + 1.0)
            grads.append(gap * (weight / skill))
            cell = skill if cell is None else cell + skill
        cell = cell / n
        for a in range(n):
            for b in range(a + 1, n):
                gap = xs[a] - xs[b]
                distance = jnp.sqrt(jnp.sum(gap * gap, axis=0, keepdims=True) * mean + 1.0)
                pull = gap * (weight / (n * distance))
                grads[a] = grads[a] - pull
                grads[b] = grads[b] + pull
                cell = cell - distance / (n * n)
        cell = cell - 1.0 / (2.0 * n)
        g_own[r] = grads[0]
        for step in range(n - 1):
            pack_rows(g_oth, (step, r), grads[step + 1], w)
        return total + weight * cell

    total = lax.fori_loop(0, band, score, jnp.zeros((1, wide), jnp.float32))
    lane = lax.broadcasted_iota(jnp.int32, (1, wide), 1)
    total = jnp.sum(jnp.where(lane < w, total, 0.0), axis=1, keepdims=True)
    loss[...] = jnp.broadcast_to(total, loss.shape)


def assemble_kernel(sizes, g_own, back, out):
    band, n, w, wide = sizes
    ens = lax.axis_index("ens")
    groups = g_own.shape[1] // GROUP
    total = out.shape[3]
    lane = lax.broadcasted_iota(jnp.int32, (g_own.shape[1], total), 1)
    span = max(total, wide)

    def one_row(r, _):
        result = None
        for step in range(n):
            if step == 0:
                cells = g_own[r]
            else:
                cells = unpack_rows(back, (step - 1, r), groups, w, wide)
            cells = jnp.concatenate([cells, jnp.zeros((cells.shape[0], span - wide), cells.dtype)], axis=1)
            owner = lax.rem(ens + step, n)
            cells = pltpu.roll(cells, owner * w, axis=1)
            mine = jnp.logical_and(lane >= owner * w, lane < (owner + 1) * w)
            result = jnp.where(mine, cells, 0.0) if result is None else jnp.where(mine, cells, result)
        out[r, 0] = result
        return 0

    lax.fori_loop(0, band, one_row, 0)


def shift_pairs(sizes, step):
    n, bands = sizes
    return [(e * bands + l, (e + step) % n * bands + l) for e in range(n) for l in range(bands)]


def halo_pairs(sizes, step, near):
    n, bands = sizes
    starts = range(0, bands - 1, 2) if near else range(1, bands - 1, 2)
    lat = [pair for i in starts for pair in ((i, i + 1), (i + 1, i))]
    return [(e * bands + a, (e + step) % n * bands + b) for e in range(n) for a, b in lat]


def per_device(members, truth, target_time, row_taps, filters, mixing):
    f32 = jnp.float32
    axes = ("ens", "lat")
    n, bands = lax.axis_size("ens"), lax.axis_size("lat")
    sizes = (n, bands)
    band, _, c, total = members.shape
    taps, kinds, lags = filters.shape[2:]
    reach2 = lags // 2
    w = total // n
    kept = w + 2 * reach2
    wide = round_up(kept, LANES)
    packed = round_up(c // GROUP * kept, LANES)
    packed_back = round_up(c // GROUP * w, LANES)
    deep = round_up(3 * taps, 4) * c
    first_row = lax.axis_index("lat") * band
    total_rows = band * bands
    ext = band + 2 * REACH

    def params(mib):
        return pltpu.CompilerParams(vmem_limit_bytes=mib * MIB)

    row = (GROUP, packed)
    own_w, near_own, far_own, oth, far_oth = pl.pallas_call(
        functools.partial(prepare_kernel, (band, n, w, reach2, wide)),
        name="prepare",
        in_specs=[VMEM],
        out_specs=[VMEM] * 5,
        out_shape=[
            jax.ShapeDtypeStruct((band, c, wide), f32),
            jax.ShapeDtypeStruct((REACH,) + row, f32),
            jax.ShapeDtypeStruct((REACH,) + row, f32),
            jax.ShapeDtypeStruct((n - 1, band) + row, f32),
            jax.ShapeDtypeStruct((n - 1, REACH) + row, f32),
        ],
        compiler_params=params(16),
    )(members)

    def along_ens(stack, sign):
        return jnp.stack(
            [lax.ppermute(stack[s - 1], axes, shift_pairs(sizes, sign * s)) for s in range(1, n)]
        )

    def halo_oth(stack, near):
        return jnp.stack(
            [lax.ppermute(stack[s - 1], axes, halo_pairs(sizes, 0 if near else s, near)) for s in range(1, n)]
        )

    oth = along_ens(oth, 1)
    far_oth = halo_oth(far_oth, False)
    far_own = lax.ppermute(far_own, axes, halo_pairs(sizes, 0, False))
    near_own = lax.ppermute(near_own, axes, halo_pairs(sizes, 0, True))

    mix = jnp.transpose(mixing[0], (1, 0, 2))
    mix = jnp.concatenate([mix, mix], axis=2)
    flat = filters[0].reshape(band * taps, kinds * lags)
    weights, target = pl.pallas_call(
        functools.partial(weights_kernel, (band, taps, lags, kinds, w, wide)),
        name="weights",
        in_specs=[SMEM, SMEM, VMEM, ANY],
        out_specs=[VMEM] * 2,
        out_shape=[
            jax.ShapeDtypeStruct((band, lags * c, deep), jnp.bfloat16),
            jax.ShapeDtypeStruct((band, c, wide), f32),
        ],
        scratch_shapes=[pltpu.VMEM((band, c, total), f32), pltpu.SemaphoreType.DMA((band,))],
        compiler_params=params(16),
    )(target_time, flat, mix, truth)

    local_taps = jnp.clip(row_taps[0] - (first_row - REACH), 0, ext - 1)
    scratch = [pltpu.VMEM((ext, 2 * c, wide), jnp.bfloat16), pltpu.VMEM((deep, wide), jnp.bfloat16)]

    odd = lax.rem(lax.axis_index("lat"), 2)
    near_oth = halo_oth(lax.dynamic_slice_in_dim(oth, 1 - odd, REACH, axis=1), True)

    x_own = pl.pallas_call(
        functools.partial(own_kernel, (band, lags, w, reach2, wide)),
        name="convolve_own",
        in_specs=[SMEM] + [VMEM] * 4,
        out_specs=VMEM,
        out_shape=jax.ShapeDtypeStruct((band, c, wide), f32),
        scratch_shapes=scratch,
        compiler_params=params(24),
    )(local_taps, weights, own_w, near_own, far_own)

    latitude = (np.arange(total_rows) + 0.5) * (math.pi / total_rows) - 0.5 * math.pi
    cosine = np.cos(latitude)
    area = lax.dynamic_slice_in_dim(jnp.asarray(cosine / cosine.mean(), f32), first_row, band)

    g_own, g_oth, loss = pl.pallas_call(
        functools.partial(score_kernel, (band, n, lags, w, reach2, wide)),
        name="score",
        in_specs=[SMEM, SMEM] + [VMEM] * 6,
        out_specs=[VMEM] * 3,
        out_shape=[
            jax.ShapeDtypeStruct((band, c, wide), f32),
            jax.ShapeDtypeStruct((n - 1, band, GROUP, packed_back), f32),
            jax.ShapeDtypeStruct((GROUP, LANES), f32),
        ],
        scratch_shapes=scratch + [pltpu.VMEM((n - 1, band, c, wide), f32)],
        compiler_params=params(24),
    )(local_taps, area, weights, x_own, oth, near_oth, far_oth, target)

    back = along_ens(g_oth, -1)
    parts = lax.all_to_all(jnp.full((n * bands,), loss[0, 0]), axes, 0, 0, tiled=True)
    loss_value = jnp.sum(parts).reshape(1) / (total_rows * total)

    score_grad = pl.pallas_call(
        functools.partial(assemble_kernel, (band, n, w, wide)),
        name="assemble",
        in_specs=[VMEM] * 2,
        out_specs=VMEM,
        out_shape=jax.ShapeDtypeStruct(members.shape, f32),
        compiler_params=params(16),
    )(g_own, back)
    return (score_grad, loss_value)


def solution(mesh):
    placed = (
        P("lat", "ens", None, None),
        P(None, "lat", None, None),
        P("lat"),
        P(None, "lat", None),
        P(None, "lat", None, None, None),
        P(),
    )
    return jax.shard_map(
        per_device,
        mesh=mesh,
        in_specs=placed,
        out_specs=(P("lat", "ens", None, None), P()),
        check_vma=False,
    )
```

time: 151 us -> 60.9 us (0.40)
  blocking collectives: 54.3 us -> 10.8 us
  matrix products: 29.4 us -> 0 us
  Pallas kernels: 0 us -> 20.8 us
  local copies, waits for them, and re-layouts: 26.8 us -> 8.44 us
  other arithmetic: 19 us -> 1.93 us
  starting transfers between devices: 11.9 us -> 6.09 us
  waiting for transfers between devices: 5.19 us -> 9.97 us
    psum x1 -> x0, blocking collectives: 54.3 us -> none  [per_device(): lax.psum(jnp.reshape(loss_part, (1,)), ('ens', 'lat')) / (total_rows * NLON)]
    dot_general x3 -> x0, matrix products: 29.4 us -> none  [the longest x1 23.5 us: per_device(): jnp.dot(coupling.reshape(band_rows * K, LW * extended_rows), shifted.resh...]
    pallas_call x0 -> x5, Pallas kernels: none -> 20.8 us  [the longest x1 6.11 us: per_device(): pl.pallas_call(functools.partial(score_kernel, (band, n, lags, w, reach2,...]
    all_to_all x0 -> x1, blocking collectives: none -> 10.8 us  [per_device(): lax.all_to_all(jnp.full((n * bands,), loss[0, 0]), axes, 0, 0, tiled=True)]
    ppermute x2 -> x6, waiting for transfers between devices: 0.83 us -> 9.97 us  [the longest x2 9.96 us: along_ens(): lax.ppermute(stack[s - 1], axes, shift_pairs(sizes, sign * s))]
    unnamed x4 -> x0, other arithmetic: 7.63 us -> none
    all_to_all x2 -> x0, starting transfers between devices: 7.37 us -> none  [the longest x1 3.8 us: per_device(): lax.all_to_all(fields, 'ens', split_axis=3, concat_axis=1, tiled=True)]
    all_to_all x6 -> x0, local copies, waits for them, and re-layouts: 5.11 us -> none  [the longest x4 2.8 us: per_device(): lax.all_to_all(fields, 'ens', split_axis=3, concat_axis=1, tiled=True)]
  transfers between devices with their start and end apart: 4 -> 6, of which waited for: 2 -> 1; matrix products, arithmetic and copies ran while one was open for 4% -> 11% of each run, Pallas kernels for 0% -> 17%
where the time goes in v1:
time: 60.9 us; the launch traced here: 60.6 us
  Pallas kernels  20.8 us (34%)
  blocking collectives  10.8 us (18%)
  waiting for transfers between devices  9.97 us (16%)
  local copies, waits for them, and re-layouts  8.44 us (14%)
  starting transfers between devices  6.09 us (10%)
  between operations  2.56 us (4%)
  other arithmetic  1.93 us (3%)
    all_to_all x1, blocking collectives, per_device(): lax.all_to_all(jnp.full((n * bands,), loss[0, 0]), axes, 0, 0, tiled=True)  10.8 us
    ppermute x2, waiting for transfers between devices, along_ens(): lax.ppermute(stack[s - 1], axes, shift_pairs(sizes, sign * s))  9.96 us
    pallas_call x1, Pallas kernels, per_device(): pl.pallas_call(functools.partial(score_kernel, (band, n, lags, w, reach2,...  6.11 us
    pallas_call x1, Pallas kernels, per_device(): pl.pallas_call(functools.partial(weights_kernel, (band, taps, lags, kinds...  5.86 us
    ppermute x2, starting transfers between devices, along_ens(): lax.ppermute(stack[s - 1], axes, shift_pairs(sizes, sign * s))  4.66 us
    pallas_call x1, Pallas kernels, per_device(): pl.pallas_call(functools.partial(own_kernel, (band, lags, w, reach2, wide...  4.5 us
    unnamed x8, local copies, waits for them, and re-layouts  3.72 us
    another operation x2, local copies, waits for them, and re-layouts, per_device(): flat = filters[0].reshape(band * taps, kinds * lags)  2.8 us
  transfers between devices with their start and end apart: 6, of which 1 were waited for; matrix products, arithmetic and copies ran while one was open for 11% of the time, Pallas kernels for 17%

profile of v1, /device:TPU:0, one launch (start us, length us, event | category | flops | bytes accessed | tf_op | source)
XLA Modules:
  0.0 60.6 jit_solution(152473978070747104)
XLA Ops:
  0.6 0.0 copy-start.1
  0.6 1.1 %copy-done.1 = f32[5,1,64,640]{3,2,1,0:T(8,128)S(1)} copy-done((f32[5,1,64,640]{3,2,1,0:T(8,128)S(1)}, f32[5,1,64,640]{3,2,1,0:T(8,128)}, u32[]{:S(2)}) %copy-start.1) | copy-done | bytes 819224
  1.8 0.0 copy-start.3
  1.8 2.5 %prepare.1 = (f32[5,64,384]{2,1,0:T(8,128)S(1)}, f32[4,8,2688]{2,1,0:T(8,128)S(1)}, f32[4,8,2688]{2,1,0:T(8,128)S(1)}, f32[1,5,8,2688]{3,2,1,0:T(8,128)S(1)}, f32[1,4,8,2688]{3,2,1,0:T(8,128)S(1)}) custom-call(f32[5,1,64,640]{3,2,1,0:T(8,128)S(1)} %copy-done.1), custom_call_target="tpu_custom_call" | custom-call | tf_op jit(solution)/shard_map/prepare/pallas_call | solution.py:348
  4.3 3.0 %collective-permute-start.2 = (f32[5,8,2688]{2,1,0:T(8,128)S(1)}, f32[5,8,2688]{2,1,0:T(8,128)S(1)}, u32[]{:S(2)}, u32[]{:S(2)}) collective-permute-start(f32[5,8,2688]{2,1,0:T(8,128)S(1)} %bitcast.18), channel_id=1, source_target_pairs={{0,16},{1,17},{2,18},{3,19},{4,20},{5,21},{6,22},{7,23},{8,24},{9,... | collective-permute-start | bytes 1290248 | tf_op jit(solution)/shard_map/ppermute | solution.py:365
  7.3 0.0 collective-permute-start
  7.3 0.7 %collective-permute-start.1 = (f32[4,8,2688]{2,1,0:T(8,128)S(1)}, f32[4,8,2688]{2,1,0:T(8,128)S(1)}, u32[]{:S(2)}, u32[]{:S(2)}) collective-permute-start(f32[4,8,2688]{2,1,0:T(8,128)S(1)} %get-tuple-element.15), channel_id=1, source_target_pairs={{1,2},{2,1},{3,4},{4,3},{5,6},{6,5},{7,8},{8,7},{9,10},{10,9},{11,... | collective-permute-start | bytes 1032200 | tf_op jit(solution)/shard_map/ppermute | solution.py:375
  8.0 0.7 %collective-permute-start.4 = (f32[4,8,2688]{2,1,0:T(8,128)S(1)}, f32[4,8,2688]{2,1,0:T(8,128)S(1)}, u32[]{:S(2)}, u32[]{:S(2)}) collective-permute-start(f32[4,8,2688]{2,1,0:T(8,128)S(1)} %bitcast.20), channel_id=1, source_target_pairs={{1,18},{2,17},{3,20},{4,19},{5,22},{6,21},{7,24},{8,23},{9,26},{10... | collective-permute-start | bytes 1032200 | tf_op jit(solution)/shard_map/ppermute | solution.py:370
  8.7 1.8 %copy.21 = f32[1,5,5,9,5]{4,3,2,1,0:T(8,128)} copy(f32[1,5,5,9,5]{3,0,4,2,1:T(1,128)} %param.11) | data formatting | bytes 9000 | tf_op jit(solution)/shard_map/reshape;squeeze | solution.py:380
  10.5 1.0 %reshape.16.filters = f32[25,45]{1,0:T(8,128)S(1)} reshape(f32[1,5,5,9,5]{4,3,2,1,0:T(8,128)} %copy.21) | data formatting | bytes 9000 | tf_op jit(solution)/shard_map/reshape;squeeze | solution.py:380
  11.5 0.7 %dynamic_slice.4.area = f32[5]{0:T(128)S(1)} dynamic-slice(f32[80]{0:T(128)} %constant.30.clone, s32[]{:T(128)S(6)} %select_n.6), dynamic_slice_sizes={5} | dynamic-slice | bytes 44 | tf_op jit(solution)/shard_map/dynamic_slice | solution.py:412
  12.2 10.0 %collective-permute-done.2 = f32[5,8,2688]{2,1,0:T(8,128)S(1)} collective-permute-done((f32[5,8,2688]{2,1,0:T(8,128)S(1)}, f32[5,8,2688]{2,1,0:T(8,128)S(1)}, u32[]{:S(2)}, u32[]{:S(2)}) %collective-permute-start.2) | collective-permute-done | bytes 430112 | tf_op jit(solution)/shard_map/ppermute | solution.py:365
  22.2 0.1 collective-permute-start.3
  22.3 1.3 %pad_maximum_fusion.mix = f32[9,64,128]{2,1,0:T(8,128)S(1)} fusion(f32[9,64,64]{2,1,0:T(8,128)} %bitcast.21), kind=kLoop, calls=%fused_computation | loop fusion | flops 73728 | bytes 442368 | tf_op jit(solution)/shard_map/concatenate | solution.py:379
  23.6 0.0 copy-start
  23.6 1.9 %copy-done = f32[4,5,64,640]{3,2,1,0:T(8,128)S(1)} copy-done((f32[4,5,64,640]{3,2,1,0:T(8,128)S(1)}, f32[4,5,64,640]{3,2,1,0:T(8,128)}, u32[]{:S(2)}) %copy-start) | copy-done | bytes 3276824
  25.5 0.0 copy-start.2
  25.5 0.7 %copy-done.2 = s32[5]{0:T(128)S(1)} copy-done((s32[5]{0:T(128)S(1)}, s32[5]{0:T(128)}, u32[]{:S(2)}) %copy-start.2) | copy-done | bytes 44
  26.2 5.9 %weights.1 = (bf16[5,320,1024]{2,1,0:T(8,128)(2,1)S(1)}, f32[5,64,384]{2,1,0:T(8,128)S(1)}) custom-call(s32[5]{0:T(128)S(1)} %copy-done.2, f32[25,45]{1,0:T(8,128)S(1)} %reshape.16.filters, f32[9,64,128]{2,1,0:T(8,128)S(1)} %pad_maximum_fusion.mix, f32[4,5,64,640]{3,2,1,0:T(8,128)S(1)} %copy-done), custom_call_target="tpu_custom_call" | custom-call | tf_op jit(solution)/shard_map/weights/pallas_call | solution.py:381
  32.0 0.0 copy-done.3
  32.1 0.0 collective-permute-done.near
  32.1 0.0 collective-permute-done.1.far
  32.1 4.5 %convolve_own.1.x_own = f32[5,64,384]{2,1,0:T(8,128)S(1)} custom-call(s32[5,5]{1,0:T(8,128)S(1)} %fusion.1.row_taps, bf16[5,320,1024]{2,1,0:T(8,128)(2,1)S(1)} %get-tuple-element.12.weights, f32[5,64,384]{2,1,0:T(8,128)S(1)} %get-tuple-element.13.own_w, f32[4,8,2688]{2,1,0:T(8,128)S(1)} %collective-permute-done.near, ...), custom_call_target="tpu_custom_call" | custom-call | tf_op jit(solution)/shard_map/convolve_own/pallas_call | solution.py:400
  36.6 0.0 collective-permute-done.4
  36.6 0.0 collective-permute-done.3
  36.6 6.1 %score.1 = (f32[5,64,384]{2,1,0:T(8,128)S(1)}, f32[1,5,8,2560]{3,2,1,0:T(8,128)S(1)}, f32[8,128]{1,0:T(8,128)S(1)}) custom-call(s32[5,5]{1,0:T(8,128)S(1)} %fusion.1.row_taps, f32[5]{0:T(128)S(1)} %dynamic_slice.4.area, bf16[5,320,1024]{2,1,0:T(8,128)(2,1)S(1)} %get-tuple-element.12.weights, f32[5,64,384]{2,1,0:T(8,128)S(1)} %convolve_own.1.x_own, ...), custom_call_target="tpu_custom_call" | custom-call | tf_op jit(solution)/shard_map/score/pallas_call | solution.py:414
  42.7 1.6 %collective-permute-start.5 = (f32[5,8,2560]{2,1,0:T(8,128)S(1)}, f32[5,8,2560]{2,1,0:T(8,128)S(1)}, u32[]{:S(2)}, u32[]{:S(2)}) collective-permute-start(f32[5,8,2560]{2,1,0:T(8,128)S(1)} %bitcast.19), channel_id=1, source_target_pairs={{0,16},{1,17},{2,18},{3,19},{4,20},{5,21},{6,22},{7,23},{8,24},{9,... | collective-permute-start | bytes 1228808 | tf_op jit(solution)/shard_map/ppermute | solution.py:365
  44.3 0.5 slice.3
  44.9 0.7 %broadcast_in_dim.3 = f32[32,1,1]{2,1,0:T(1,128)S(1)} broadcast(f32[]{:T(128)} %bitcast.10), dimensions={} | broadcast | bytes 132 | tf_op jit(solution)/shard_map/broadcast_in_dim | solution.py:429
  45.5 10.8 %all_to_all.6 = f32[32,1,1]{2,1,0:T(1,128)S(1)} all-to-all(f32[32,1,1]{2,1,0:T(1,128)S(1)} %broadcast_in_dim.3), channel_id=1, replica_groups=mesh['ens'=2,'lat'=16] {'ens','lat'}, dimensions={0} | all-to-all | bytes 256 | tf_op jit(solution)/shard_map/all_to_all | solution.py:429
  56.3 0.6 %reduce_sum.9 = f32[]{:T(128)} reduce(f32[32,1,1]{2,1,0:T(1,128)S(1)} %all_to_all.6, f32[]{:T(128)} %constant.28.clone.1), dimensions={0,1,2}, to_apply=%region_0.1 | reduce | flops 31 | bytes 136 | tf_op jit(solution)/shard_map/reduce_sum | solution.py:430
  57.6 0.0 collective-permute-done.5
  57.6 1.8 %assemble.1 = f32[5,1,64,640]{3,2,1,0:T(8,128)} custom-call(f32[5,64,384]{2,1,0:T(8,128)S(1)} %get-tuple-element.19.g_own, f32[1,5,8,2560]{3,2,1,0:T(8,128)S(1)} %bitcast.15), custom_call_target="tpu_custom_call" | custom-call | tf_op jit(solution)/shard_map/assemble/pallas_call | solution.py:432
  (2 shorter events, 0.0 us)
Async XLA Ops:
  0.6 1.1 %copy-start.1 = (f32[5,1,64,640]{3,2,1,0:T(8,128)S(1)}, f32[5,1,64,640]{3,2,1,0:T(8,128)}, u32[]{:S(2)}) copy-start(f32[5,1,64,640]{3,2,1,0:T(8,128)} %members.1) | copy-start | bytes 2457604
  1.8 30.3 %copy-start.3 = (s32[1,5,5]{2,0,1:T(1,128)S(1)}, s32[1,5,5]{2,0,1:T(1,128)}, u32[]{:S(2)}) copy-start(s32[1,5,5]{2,0,1:T(1,128)} %param.10) | copy-start | bytes 304
  4.3 17.9 %collective-permute-start.2 = (f32[5,8,2688]{2,1,0:T(8,128)S(1)}, f32[5,8,2688]{2,1,0:T(8,128)S(1)}, u32[]{:S(2)}, u32[]{:S(2)}) collective-permute-start(f32[5,8,2688]{2,1,0:T(8,128)S(1)} %bitcast.18), channel_id=1, source_target_pairs={{0,16},{1,17},{2,18},{3,19},{4,20},{5,21},{6,22},{7,23},{8,24},{9,... | collective-permute-start | bytes 1290248 | tf_op jit(solution)/shard_map/ppermute | solution.py:365
  7.3 24.8 %collective-permute-start = (f32[4,8,2688]{2,1,0:T(8,128)S(1)}, f32[4,8,2688]{2,1,0:T(8,128)S(1)}, u32[]{:S(2)}, u32[]{:S(2)}) collective-permute-start(f32[4,8,2688]{2,1,0:T(8,128)S(1)} %get-tuple-element.14), channel_id=1, source_target_pairs={{0,1},{1,0},{2,3},{3,2},{4,5},{5,4},{6,7},{7,6},{8,9},{9,8},{10,11... | collective-permute-start | bytes 1032200 | tf_op jit(solution)/shard_map/ppermute | solution.py:376
  7.3 24.8 %collective-permute-start.1 = (f32[4,8,2688]{2,1,0:T(8,128)S(1)}, f32[4,8,2688]{2,1,0:T(8,128)S(1)}, u32[]{:S(2)}, u32[]{:S(2)}) collective-permute-start(f32[4,8,2688]{2,1,0:T(8,128)S(1)} %get-tuple-element.15), channel_id=1, source_target_pairs={{1,2},{2,1},{3,4},{4,3},{5,6},{6,5},{7,8},{8,7},{9,10},{10,9},{11,... | collective-permute-start | bytes 1032200 | tf_op jit(solution)/shard_map/ppermute | solution.py:375
  8.0 28.6 %collective-permute-start.4 = (f32[4,8,2688]{2,1,0:T(8,128)S(1)}, f32[4,8,2688]{2,1,0:T(8,128)S(1)}, u32[]{:S(2)}, u32[]{:S(2)}) collective-permute-start(f32[4,8,2688]{2,1,0:T(8,128)S(1)} %bitcast.20), channel_id=1, source_target_pairs={{1,18},{2,17},{3,20},{4,19},{5,22},{6,21},{7,24},{8,23},{9,26},{10... | collective-permute-start | bytes 1032200 | tf_op jit(solution)/shard_map/ppermute | solution.py:370
  22.2 14.4 %collective-permute-start.3 = (f32[4,8,2688]{2,1,0:T(8,128)S(1)}, f32[4,8,2688]{2,1,0:T(8,128)S(1)}, u32[]{:S(2)}, u32[]{:S(2)}) collective-permute-start(f32[4,8,2688]{2,1,0:T(8,128)S(1)} %constant_dynamic-slice_fusion), channel_id=1, source_target_pairs={{0,1},{1,0},{2,3},{3,2},{4,5},{5,4},{6,7},{7,6},{8,9},{9,8},{10,11... | collective-permute-start | bytes 1032200 | tf_op jit(solution)/shard_map/ppermute | solution.py:370
  23.6 1.9 %copy-start = (f32[4,5,64,640]{3,2,1,0:T(8,128)S(1)}, f32[4,5,64,640]{3,2,1,0:T(8,128)}, u32[]{:S(2)}) copy-start(f32[4,5,64,640]{3,2,1,0:T(8,128)} %truth.1) | copy-start | bytes 9830404
  25.5 0.7 %copy-start.2 = (s32[5]{0:T(128)S(1)}, s32[5]{0:T(128)}, u32[]{:S(2)}) copy-start(s32[5]{0:T(128)} %times.1) | copy-start | bytes 64
  42.7 14.9 %collective-permute-start.5 = (f32[5,8,2560]{2,1,0:T(8,128)S(1)}, f32[5,8,2560]{2,1,0:T(8,128)S(1)}, u32[]{:S(2)}, u32[]{:S(2)}) collective-permute-start(f32[5,8,2560]{2,1,0:T(8,128)S(1)} %bitcast.19), channel_id=1, source_target_pairs={{0,16},{1,17},{2,18},{3,19},{4,20},{5,21},{6,22},{7,23},{8,24},{9,... | collective-permute-start | bytes 1228808 | tf_op jit(solution)/shard_map/ppermute | solution.py:365

commit v2 on v1

v2 whole, which is shorter than its diff:
```python
import functools
import math

import jax
import jax.numpy as jnp
import numpy as np
from jax import lax
from jax.experimental import pallas as pl
from jax.experimental.pallas import tpu as pltpu
from jax.sharding import PartitionSpec as P


REACH = 4
LANES = 128
GROUP = 8
MIB = 1 << 20

VMEM = pl.BlockSpec(memory_space=pltpu.VMEM)
SMEM = pl.BlockSpec(memory_space=pltpu.SMEM)
HBM = pl.BlockSpec(memory_space=pltpu.MemorySpace.HBM)


def round_up(value, unit):
    return -(-value // unit) * unit


def shift_left(cells, amount):
    width = cells.shape[-1]
    amount %= width
    return cells if amount == 0 else pltpu.roll(cells, width - amount, axis=cells.ndim - 1)


def pack_tiles(cells, width, start=0):
    groups = cells.shape[0] // GROUP
    lane = lax.broadcasted_iota(jnp.int32, (GROUP, LANES), 1)
    tiles = []
    for group in range(groups):
        part = cells[group * GROUP : (group + 1) * GROUP]
        offset = group * width % LANES
        count = -(-(offset + width) // LANES)
        pad = count * LANES - part.shape[1]
        if pad > 0:
            part = jnp.concatenate([part, jnp.zeros((GROUP, pad), part.dtype)], axis=1)
        part = shift_left(part, start - offset)
        values = [part[:, i * LANES : (i + 1) * LANES] for i in range(count)]
        if offset:
            values[0] = jnp.where(lane < offset, tiles.pop(), values[0])
        tiles += values
    return tiles


def store_tiles(ref, at, tiles):
    for i, tile in enumerate(tiles):
        ref[at + (slice(None), pl.ds(i * LANES, LANES))] = tile


def unpack_rows(ref, at, groups, width, wide):
    parts = []
    limit = ref.shape[-1]
    for group in range(groups):
        first = group * width
        offset = first % LANES
        base = first - offset
        take = min(wide + (LANES if offset else 0), limit - base)
        part = ref[at + (slice(None), pl.ds(base, take))]
        if take < wide:
            part = jnp.concatenate([part, jnp.zeros((GROUP, wide - take), part.dtype)], axis=1)
        if offset:
            part = shift_left(part, offset)
        parts.append(part[:, :wide])
    return jnp.concatenate(parts, axis=0)


def gelu(v):
    return 0.5 * v * (1.0 + jnp.tanh(math.sqrt(2.0 / math.pi) * (v + 0.044715 * (v * v * v))))


def prepare_kernel(sizes, members, own_w, near_own, far_own, oth, far_oth):
    band, n, w, reach2, wide = sizes
    ens = lax.axis_index("ens")
    odd = lax.rem(lax.axis_index("lat"), 2)
    kept = w + 2 * reach2
    near_from, far_from = 1 - odd, odd
    for p in range(n):
        start = p * w - reach2

        @pl.when(ens != p)
        def _():
            step = lax.rem(p - ens + n, n) - 1
            for r in range(band):
                tiles = pack_tiles(members[r, 0], kept, start)
                store_tiles(oth, (step, r), tiles)
                far_at = r - far_from

                @pl.when(jnp.logical_and(far_at >= 0, far_at < REACH))
                def _():
                    store_tiles(far_oth, (step, far_at), tiles)

        @pl.when(ens == p)
        def _():
            for r in range(band):
                row = members[r, 0]
                own_w[r] = shift_left(row, start)[:, :wide]
                tiles = pack_tiles(row, kept, start)
                near_at, far_at = r - near_from, r - far_from

                @pl.when(jnp.logical_and(near_at >= 0, near_at < REACH))
                def _():
                    store_tiles(near_own, (near_at,), tiles)

                @pl.when(jnp.logical_and(far_at >= 0, far_at < REACH))
                def _():
                    store_tiles(far_own, (far_at,), tiles)


def weights_kernel(sizes, times, filters, mix, truth, weights, target, twice, held, sems):
    band, n, taps, lags, kinds, w, wide = sizes
    copies = [pltpu.make_async_copy(truth.at[times[r], r], held.at[r], sems.at[r]) for r in range(band)]
    for copy in copies:
        copy.start()
    c = mix.shape[1]
    half = lax.broadcasted_iota(jnp.int32, (c, 2 * c), 1) < c
    for k in range(kinds):
        twice[k] = jnp.concatenate([mix[k], mix[k]], axis=1)

    def one_row(r, _):
        for d in range(lags):
            for t in range(0, taps, 2):
                acc = None
                for k in range(kinds):
                    scale = filters[r, t, d, 0, k]
                    if t + 1 < taps:
                        scale = jnp.where(half[:GROUP], scale, filters[r, t + 1, d, 0, k])
                        scale = jnp.concatenate([scale] * (c // GROUP), axis=0)
                    term = scale * twice[k]
                    acc = term if acc is None else acc + term
                high = acc.astype(jnp.bfloat16).astype(jnp.float32)
                low = acc - high
                if t + 1 < taps:
                    blocks = [high, low, high]
                else:
                    blocks = [jnp.where(half, high, low), jnp.where(half, high, 0.0)]
                for i, block in enumerate(blocks):
                    at = (3 * (t // 2) + i) * 2 * c
                    weights[r, pl.ds(d * c, c), pl.ds(at, 2 * c)] = block.astype(jnp.bfloat16)
        return 0

    lax.fori_loop(0, band, one_row, 0)
    ens = lax.axis_index("ens")
    for copy in copies:
        copy.wait()
    for p in range(n):

        @pl.when(ens == p)
        def _():
            for r in range(band):
                target[r] = shift_left(held[r], p * w)[:, :wide]


def store_split(split, q, cells):
    c = cells.shape[0]
    high = cells.astype(jnp.bfloat16)
    split[q, pl.ds(0, c)] = high
    split[q, pl.ds(c, c)] = (cells - high.astype(jnp.float32)).astype(jnp.bfloat16)


def store_halo(split, near, near_at, far, far_at, kept, wide, band):
    odd = lax.rem(lax.axis_index("lat"), 2)
    groups = split.shape[-2] // 2 // GROUP
    low_base = REACH + band
    for ref, at, base in ((near, near_at, low_base * (1 - odd)), (far, far_at, low_base * odd)):
        if ref is not None:
            for i in range(REACH):
                store_split(split, i + base, unpack_rows(ref, at + (i,), groups, kept, wide))


def tap_rows(row_taps, r, band, ext):
    first = lax.axis_index("lat") * band - REACH
    return [
        jnp.clip(row_taps[r, 0, t] - first, 0, ext - 1) for t in range(row_taps.shape[2])
    ]


def convolve(row_taps, weights, split, r, lags, band):
    c = split.shape[1] // 2
    rows = tap_rows(row_taps, r, band, split.shape[0])
    blocks = []
    for t in range(0, len(rows), 2):
        pair = rows[t : t + 2]
        high = [split[q, pl.ds(0, c)] for q in pair]
        low = [split[q, pl.ds(c, c)] for q in pair]
        blocks += high + high + low
        if len(pair) == 1:
            blocks.append(jnp.zeros_like(low[0]))
    stack = jnp.concatenate(blocks, axis=0)
    products = jnp.dot(weights[r], stack, preferred_element_type=jnp.float32)
    mixed = products[0:c]
    for d in range(1, lags):
        mixed = mixed + shift_left(products[d * c : (d + 1) * c], d)
    return mixed


def own_kernel(sizes, row_taps, weights, own_w, near, far, x_own, split):
    band, lags, w, reach2, wide = sizes
    kept = w + 2 * reach2
    store_halo(split, near, (), far, (), kept, wide, band)
    for r in range(band):
        store_split(split, REACH + r, own_w[r])
    for r in range(band):
        mixed = convolve(row_taps, weights, split, r, lags, band)
        x_own[r] = shift_left(own_w[r], reach2) + gelu(mixed)


def receive_kernel(sizes, oth, near, states, split):
    band, n, w, reach2, wide = sizes
    first = 1 - lax.rem(lax.axis_index("lat"), 2)
    for step in range(n - 1):
        for i in range(REACH):
            near[step, i] = oth[step, first + i]
    kept = w + 2 * reach2
    groups = states.shape[2] // GROUP
    for step in range(n - 1):
        for r in range(band):
            cells = unpack_rows(oth, (step, r), groups, kept, wide)
            store_split(split.at[step], REACH + r, cells)
            states[step, r] = shift_left(cells, reach2)


def score_kernel(
    sizes, row_taps, area, weights, x_own, states, near, far, target, split_in, g_own, g_oth, parts, split
):
    band, n, lags, w, reach2, wide = sizes
    kept = w + 2 * reach2
    c = x_own.shape[1]
    first_row = lax.axis_index("lat") * band
    for step in range(n - 1):
        store_halo(split.at[step], near, (step,), far, (step,), kept, wide, band)

    def other_state(step, r):
        return states[step, r] + gelu(convolve(row_taps, weights, split.at[step], r, lags, band))

    def score(r, total):
        weight = area[first_row + r]
        truth = target[r]
        xs = [x_own[r]] + [other_state(step, r) for step in range(n - 1)]
        mean = 1.0 / c
        cell = None
        grads = []
        for x in xs:
            gap = x - truth
            skill = jnp.sqrt(jnp.sum(gap * gap, axis=0, keepdims=True) * mean + 1.0)
            grads.append(gap * (weight / skill))
            cell = skill if cell is None else cell + skill
        cell = cell / n
        for a in range(n):
            for b in range(a + 1, n):
                gap = xs[a] - xs[b]
                distance = jnp.sqrt(jnp.sum(gap * gap, axis=0, keepdims=True) * mean + 1.0)
                pull = gap * (weight / (n * distance))
                grads[a] = grads[a] - pull
                grads[b] = grads[b] + pull
                cell = cell - distance / (n * n)
        cell = cell - 1.0 / (2.0 * n)
        g_own[r] = grads[0]
        for step in range(n - 1):
            store_tiles(g_oth, (step, r), pack_tiles(grads[step + 1], w))
        return total + weight * cell

    total = jnp.zeros((1, wide), jnp.float32)
    for r in range(band):
        total = score(r, total)
    lane = lax.broadcasted_iota(jnp.int32, (1, wide), 1)
    total = jnp.sum(jnp.where(lane < w, total, 0.0), axis=1, keepdims=True)
    parts[...] = jnp.broadcast_to(total[None], parts.shape)


def assemble_kernel(sizes, g_own, back, parts, out, loss):
    band, n, w, wide = sizes
    ens = lax.axis_index("ens")
    groups = g_own.shape[1] // GROUP
    total = out.shape[3]
    lane = lax.broadcasted_iota(jnp.int32, (g_own.shape[1], total), 1)
    span = max(total, wide)

    def one_row(r, _):
        result = None
        for step in range(n):
            if step == 0:
                cells = g_own[r]
            else:
                cells = unpack_rows(back, (step - 1, r), groups, w, wide)
            cells = jnp.concatenate([cells, jnp.zeros((cells.shape[0], span - wide), cells.dtype)], axis=1)
            owner = lax.rem(ens + step, n)
            cells = pltpu.roll(cells, owner * w, axis=1)
            mine = jnp.logical_and(lane >= owner * w, lane < (owner + 1) * w)
            result = jnp.where(mine, cells, 0.0) if result is None else jnp.where(mine, cells, result)
        out[r, 0] = result
        return 0

    lax.fori_loop(0, band, one_row, 0)
    cells = band * (parts.shape[0] // n) * total
    loss[0] = jnp.sum(jnp.sum(parts[...], axis=0)[:, :1]) / cells


def shift_pairs(sizes, step):
    n, bands = sizes
    return [(e * bands + l, (e + step) % n * bands + l) for e in range(n) for l in range(bands)]


def halo_pairs(sizes, step, near):
    n, bands = sizes
    starts = range(0, bands - 1, 2) if near else range(1, bands - 1, 2)
    lat = [pair for i in starts for pair in ((i, i + 1), (i + 1, i))]
    return [(e * bands + a, (e + step) % n * bands + b) for e in range(n) for a, b in lat]


def per_device(members, truth, target_time, row_taps, filters, mixing):
    f32 = jnp.float32
    axes = ("ens", "lat")
    n, bands = lax.axis_size("ens"), lax.axis_size("lat")
    sizes = (n, bands)
    band, _, c, total = members.shape
    taps, kinds, lags = filters.shape[2:]
    reach2 = lags // 2
    row_taps = jnp.transpose(row_taps, (1, 0, 2))
    filters = jnp.transpose(filters, (1, 2, 4, 0, 3))
    mix = jnp.transpose(mixing[0], (1, 0, 2))
    w = total // n
    kept = w + 2 * reach2
    wide = round_up(kept, LANES)
    packed = round_up(c // GROUP * kept, LANES)
    packed_back = round_up(c // GROUP * w, LANES)
    deep = (3 * (taps // 2) + 2 * (taps % 2)) * 2 * c
    total_rows = band * bands
    ext = band + 2 * REACH

    def params(mib):
        return pltpu.CompilerParams(vmem_limit_bytes=mib * MIB)

    def takes(micros):
        return pl.CostEstimate(flops=0, bytes_accessed=int(micros * 3.69e6), transcendentals=0)

    row = (GROUP, packed)
    own_w, near_own, far_own, oth, far_oth = pl.pallas_call(
        functools.partial(prepare_kernel, (band, n, w, reach2, wide)),
        name="prepare",
        cost_estimate=takes(1.2),
        in_specs=[VMEM],
        out_specs=[VMEM] * 5,
        out_shape=[
            jax.ShapeDtypeStruct((band, c, wide), f32),
            jax.ShapeDtypeStruct((REACH,) + row, f32),
            jax.ShapeDtypeStruct((REACH,) + row, f32),
            jax.ShapeDtypeStruct((n - 1, band) + row, f32),
            jax.ShapeDtypeStruct((n - 1, REACH) + row, f32),
        ],
        compiler_params=params(16),
    )(members)

    def along_ens(stack, sign):
        return jnp.stack(
            [lax.ppermute(stack[s - 1], axes, shift_pairs(sizes, sign * s)) for s in range(1, n)]
        )

    def halo_oth(stack, near):
        return jnp.stack(
            [lax.ppermute(stack[s - 1], axes, halo_pairs(sizes, 0 if near else s, near)) for s in range(1, n)]
        )

    oth = along_ens(oth, 1)
    far_own = lax.ppermute(far_own, axes, halo_pairs(sizes, 0, False))
    near_own = lax.ppermute(near_own, axes, halo_pairs(sizes, 0, True))
    far_oth = halo_oth(far_oth, False)

    weights, target = pl.pallas_call(
        functools.partial(weights_kernel, (band, n, taps, lags, kinds, w, wide)),
        name="weights",
        cost_estimate=takes(4.0),
        in_specs=[SMEM, SMEM, VMEM, HBM],
        out_specs=[VMEM] * 2,
        out_shape=[
            jax.ShapeDtypeStruct((band, lags * c, deep), jnp.bfloat16),
            jax.ShapeDtypeStruct((band, c, wide), f32),
        ],
        scratch_shapes=[
            pltpu.VMEM((kinds, c, 2 * c), f32),
            pltpu.VMEM((band, c, total), f32),
            pltpu.SemaphoreType.DMA((band,)),
        ],
        compiler_params=params(47),
    )(target_time, filters, mix, truth)

    split_shape = jax.ShapeDtypeStruct((n - 1, ext, 2 * c, wide), jnp.bfloat16)

    split_shape = jax.ShapeDtypeStruct((n - 1, ext, 2 * c, wide), jnp.bfloat16)

    split_shape = jax.ShapeDtypeStruct((n - 1, ext, 2 * c, wide), jnp.bfloat16)

    split_shape = jax.ShapeDtypeStruct((n - 1, ext, 2 * c, wide), jnp.bfloat16)

    x_own = pl.pallas_call(
        functools.partial(own_kernel, (band, lags, w, reach2, wide)),
        name="convolve_own",
        cost_estimate=takes(3.0),
        in_specs=[SMEM] + [VMEM] * 4,
        out_specs=VMEM,
        out_shape=jax.ShapeDtypeStruct((band, c, wide), f32),
        scratch_shapes=[pltpu.VMEM((ext, 2 * c, wide), jnp.bfloat16)],
        compiler_params=params(24),
    )(row_taps, weights, own_w, near_own, far_own)

    near_oth, states, split_oth = pl.pallas_call(
        functools.partial(receive_kernel, (band, n, w, reach2, wide)),
        name="receive",
        cost_estimate=takes(0.6),
        in_specs=[VMEM],
        out_specs=[VMEM] * 3,
        out_shape=[
            jax.ShapeDtypeStruct((n - 1, REACH) + row, f32),
            jax.ShapeDtypeStruct((n - 1, band, c, wide), f32),
            split_shape,
        ],
        compiler_params=params(24),
    )(oth)
    near_oth = halo_oth(near_oth, True)

    latitude = (np.arange(total_rows) + 0.5) * (math.pi / total_rows) - 0.5 * math.pi
    cosine = np.cos(latitude)
    area = jnp.asarray(cosine / cosine.mean(), f32)

    g_own, g_oth, parts, _ = pl.pallas_call(
        functools.partial(score_kernel, (band, n, lags, w, reach2, wide)),
        name="score",
        cost_estimate=takes(3.1),
        in_specs=[SMEM, SMEM] + [VMEM] * 7,
        out_specs=[VMEM] * 4,
        out_shape=[
            jax.ShapeDtypeStruct((band, c, wide), f32),
            jax.ShapeDtypeStruct((n - 1, band, GROUP, packed_back), f32),
            jax.ShapeDtypeStruct((n * bands, 1, LANES), f32),
            split_shape,
        ],
        input_output_aliases={8: 3},
        compiler_params=params(24),
    )(row_taps, area, weights, x_own, states, near_oth, far_oth, target, split_oth)

    back = along_ens(g_oth, -1)
    parts = lax.all_to_all(parts, axes, 0, 0, tiled=True)

    score_grad, loss_value = pl.pallas_call(
        functools.partial(assemble_kernel, (band, n, w, wide)),
        name="assemble",
        cost_estimate=takes(1.8),
        in_specs=[VMEM] * 3,
        out_specs=[VMEM, SMEM],
        out_shape=[jax.ShapeDtypeStruct(members.shape, f32), jax.ShapeDtypeStruct((1,), f32)],
        compiler_params=params(16),
    )(g_own, back, parts)
    return (score_grad, loss_value)


def solution(mesh):
    placed = (
        P("lat", "ens", None, None),
        P(None, "lat", None, None),
        P("lat"),
        P(None, "lat", None),
        P(None, "lat", None, None, None),
        P(),
    )
    return jax.shard_map(
        per_device,
        mesh=mesh,
        in_specs=placed,
        out_specs=(P("lat", "ens", None, None), P()),
        check_vma=False,
    )
```

time: 60.9 us -> 48.8 us (0.80)
  Pallas kernels: 20.8 us -> 13.6 us
  local copies, waits for them, and re-layouts: 8.44 us -> 3.59 us
  waiting for transfers between devices: 9.97 us -> 13.5 us
  other arithmetic: 1.93 us -> 0 us
  between operations: 2.56 us -> 0.77 us
    ppermute x2, waiting for transfers between devices: 9.96 us -> 13.5 us  [along_ens(): lax.ppermute(stack[s - 1], axes, shift_pairs(sizes, sign * s))]
    pallas_call x1, Pallas kernels: 6.11 us -> 3.13 us  [per_device(): pl.pallas_call(functools.partial(score_kernel, (band, n, lags, w, reach2,...]
    another operation x2 -> x0, local copies, waits for them, and re-layouts: 2.8 us -> none  [per_device(): flat = filters[0].reshape(band * taps, kinds * lags)]
    pallas_call x1, Pallas kernels: 4.5 us -> 2.95 us  [per_device(): pl.pallas_call(functools.partial(own_kernel, (band, lags, w, reach2, wide...]
    pallas_call x1 -> x2, Pallas kernels: 5.86 us -> 4.51 us  [the longest x1 3.91 us: per_device(): pl.pallas_call(functools.partial(weights_kernel, (band, n, taps, lags, ki...]
    pallas_call x1, Pallas kernels: 2.48 us -> 1.16 us  [per_device(): pl.pallas_call(functools.partial(prepare_kernel, (band, n, w, reach2, wid...]
    concatenate x1 -> x0, other arithmetic: 1.28 us -> none  [per_device(): mix = jnp.concatenate([mix, mix], axis=2)]
    dynamic_slice x1 -> x0, local copies, waits for them, and re-layouts: 0.74 us -> none  [per_device(): lax.dynamic_slice_in_dim(jnp.asarray(cosine / cosine.mean(), f32), first_...]
  transfers between devices with their start and end apart: 6 -> 6, of which waited for: 1 -> 1; matrix products, arithmetic and copies ran while one was open for 11% -> 0% of each run, Pallas kernels for 17% -> 15%
where the time goes in v2:
time: 48.8 us; the launch traced here: 48.6 us
  Pallas kernels  13.6 us (28%)
  waiting for transfers between devices  13.5 us (28%)
  blocking collectives  10.8 us (22%)
  starting transfers between devices  6.32 us (13%)
  local copies, waits for them, and re-layouts  3.59 us (7%)
  between operations  0.77 us (2%)
    ppermute x2, waiting for transfers between devices, along_ens(): lax.ppermute(stack[s - 1], axes, shift_pairs(sizes, sign * s))  13.5 us
    all_to_all x1, blocking collectives, per_device(): parts = lax.all_to_all(parts, axes, 0, 0, tiled=True)  10.8 us
    ppermute x2, starting transfers between devices, along_ens(): lax.ppermute(stack[s - 1], axes, shift_pairs(sizes, sign * s))  4.89 us
    pallas_call x1, Pallas kernels, per_device(): pl.pallas_call(functools.partial(weights_kernel, (band, n, taps, lags, ki...  3.91 us
    unnamed x12, local copies, waits for them, and re-layouts  3.59 us
    pallas_call x1, Pallas kernels, per_device(): pl.pallas_call(functools.partial(score_kernel, (band, n, lags, w, reach2,...  3.13 us
    pallas_call x1, Pallas kernels, per_device(): pl.pallas_call(functools.partial(own_kernel, (band, lags, w, reach2, wide...  2.95 us
    pallas_call x1, Pallas kernels, per_device(): pl.pallas_call(functools.partial(assemble_kernel, (band, n, w, wide)), na...  1.85 us
  transfers between devices with their start and end apart: 6, of which 1 were waited for; matrix products, arithmetic and copies ran while one was open for 0% of the time, Pallas kernels for 15%

profile of v2, /device:TPU:0, one launch (start us, length us, event | category | flops | bytes accessed | tf_op | source)
XLA Modules:
  0.0 48.6 jit_solution(14875304127485347957)
XLA Ops:
  0.6 0.0 copy-start
  0.6 1.1 %copy-done = f32[5,1,64,640]{3,2,1,0:T(8,128)S(1)} copy-done((f32[5,1,64,640]{3,2,1,0:T(8,128)S(1)}, f32[5,1,64,640]{3,2,1,0:T(8,128)}, u32[]{:S(2)}) %copy-start) | copy-done | bytes 819224
  1.8 0.0 copy-start.3
  1.8 1.2 %prepare.1 = (f32[5,64,384]{2,1,0:T(8,128)S(1)}, f32[4,8,2688]{2,1,0:T(8,128)S(1)}, f32[4,8,2688]{2,1,0:T(8,128)S(1)}, f32[1,5,8,2688]{3,2,1,0:T(8,128)S(1)}, f32[1,4,8,2688]{3,2,1,0:T(8,128)S(1)}) custom-call(f32[5,1,64,640]{3,2,1,0:T(8,128)S(1)} %copy-done), custom_call_target="tpu_custom_call" | custom-call | bytes 4428000 | tf_op jit(solution)/shard_map/prepare/pallas_call | solution.py:344
  2.9 3.0 %collective-permute-start.2 = (f32[5,8,2688]{2,1,0:T(8,128)S(1)}, f32[5,8,2688]{2,1,0:T(8,128)S(1)}, u32[]{:S(2)}, u32[]{:S(2)}) collective-permute-start(f32[5,8,2688]{2,1,0:T(8,128)S(1)} %bitcast.21), channel_id=1, source_target_pairs={{0,16},{1,17},{2,18},{3,19},{4,20},{5,21},{6,22},{7,23},{8,24},{9,... | collective-permute-start | bytes 1290248 | tf_op jit(solution)/shard_map/ppermute | solution.py:362
  6.0 0.0 collective-permute-start
  6.0 0.7 %collective-permute-start.1 = (f32[4,8,2688]{2,1,0:T(8,128)S(1)}, f32[4,8,2688]{2,1,0:T(8,128)S(1)}, u32[]{:S(2)}, u32[]{:S(2)}) collective-permute-start(f32[4,8,2688]{2,1,0:T(8,128)S(1)} %get-tuple-element.18), channel_id=1, source_target_pairs={{1,2},{2,1},{3,4},{4,3},{5,6},{6,5},{7,8},{8,7},{9,10},{10,9},{11,... | collective-permute-start | bytes 1032200 | tf_op jit(solution)/shard_map/ppermute | solution.py:371
  6.7 0.7 %collective-permute-start.4 = (f32[4,8,2688]{2,1,0:T(8,128)S(1)}, f32[4,8,2688]{2,1,0:T(8,128)S(1)}, u32[]{:S(2)}, u32[]{:S(2)}) collective-permute-start(f32[4,8,2688]{2,1,0:T(8,128)S(1)} %bitcast.23), channel_id=1, source_target_pairs={{1,18},{2,17},{3,20},{4,19},{5,22},{6,21},{7,24},{8,23},{9,26},{10... | collective-permute-start | bytes 1032200 | tf_op jit(solution)/shard_map/ppermute | solution.py:367
  7.4 13.5 %collective-permute-done.2 = f32[5,8,2688]{2,1,0:T(8,128)S(1)} collective-permute-done((f32[5,8,2688]{2,1,0:T(8,128)S(1)}, f32[5,8,2688]{2,1,0:T(8,128)S(1)}, u32[]{:S(2)}, u32[]{:S(2)}) %collective-permute-start.2) | collective-permute-done | bytes 430112 | tf_op jit(solution)/shard_map/ppermute | solution.py:362
  20.9 0.6 %receive.1 = (f32[1,4,8,2688]{3,2,1,0:T(8,128)S(1)}, f32[1,5,64,384]{3,2,1,0:T(8,128)S(1)}, bf16[1,13,128,384]{3,2,1,0:T(8,128)(2,1)S(1)}) custom-call(f32[1,5,8,2688]{3,2,1,0:T(8,128)S(1)} %bitcast.13), custom_call_target="tpu_custom_call" | custom-call | bytes 2214000 | tf_op jit(solution)/shard_map/receive/pallas_call | solution.py:412
  21.5 0.1 collective-permute-start.3
  21.6 0.0 copy-start.1
  21.6 1.0 %copy-done.1 = f32[1,64,9,64]{3,1,2,0:T(8,128)S(1)} copy-done((f32[1,64,9,64]{3,1,2,0:T(8,128)S(1)}, f32[1,64,9,64]{3,1,2,0:T(8,128)}, u32[]{:S(2)}) %copy-start.1) | copy-done | bytes 147480
  22.5 0.0 copy-start.2
  22.5 0.8 %copy-done.2 = f32[1,5,5,9,5]{3,0,4,2,1:T(1,128)S(1)} copy-done((f32[1,5,5,9,5]{3,0,4,2,1:T(1,128)S(1)}, f32[1,5,5,9,5]{3,0,4,2,1:T(1,128)}, u32[]{:S(2)}) %copy-start.2) | copy-done | bytes 4524
  23.4 0.0 copy-start.4
  23.4 0.7 %copy-done.4 = s32[5]{0:T(128)S(1)} copy-done((s32[5]{0:T(128)S(1)}, s32[5]{0:T(128)}, u32[]{:S(2)}) %copy-start.4) | copy-done | bytes 44
  24.0 3.9 %weights.1 = (bf16[5,320,1024]{2,1,0:T(8,128)(2,1)S(1)}, f32[5,64,384]{2,1,0:T(8,128)S(1)}) custom-call(s32[5]{0:T(128)S(1)} %copy-done.4, f32[5,5,5,1,9]{4,3,2,1,0:T(1,128)S(1)} %bitcast.18, f32[9,64,64]{2,1,0:T(8,128)S(1)} %bitcast.17, f32[4,5,64,640]{3,2,1,0:T(8,128)} %truth.1), custom_call_target="tpu_custom_call" | custom-call | bytes 14760000 | tf_op jit(solution)/shard_map/weights/pallas_call | solution.py:375
  27.9 0.0 copy-start.5
  27.9 0.0 collective-permute-done.near
  27.9 0.0 collective-permute-done.1.far
  28.0 0.0 copy-done.3
  28.0 3.0 %convolve_own.1.x_own = f32[5,64,384]{2,1,0:T(8,128)S(1)} custom-call(s32[5,1,5]{2,1,0:T(1,128)S(1)} %bitcast.19, bf16[5,320,1024]{2,1,0:T(8,128)(2,1)S(1)} %get-tuple-element.15.weights, f32[5,64,384]{2,1,0:T(8,128)S(1)} %get-tuple-element.16.own_w, f32[4,8,2688]{2,1,0:T(8,128)S(1)} %collective-permute-done.near, f32[4,8,2688]{2,1,0:T(8,128)S(1)} %collective-permute-done.1.far), custom_call_target="tpu_custom_call" | custom-call | bytes 11070000 | tf_op jit(solution)/shard_map/convolve_own/pallas_call | solution.py:401
  30.9 0.0 collective-permute-done.4
  30.9 0.0 collective-permute-done.3
  31.0 0.0 copy-done.5
  31.0 3.1 %score.1 = (f32[5,64,384]{2,1,0:T(8,128)S(1)}, f32[1,5,8,2560]{3,2,1,0:T(8,128)S(1)}, f32[32,1,128]{2,1,0:T(1,128)S(1)}, bf16[1,13,128,384]{3,2,1,0:T(8,128)(2,1)S(1)}) custom-call(s32[5,1,5]{2,1,0:T(1,128)S(1)} %bitcast.20, f32[80]{0:T(128)S(1)} %copy-done.5, bf16[5,320,1024]{2,1,0:T(8,128)(2,1)S(1)} %get-tuple-element.15.weights, ...), custom_call_target="tpu_custom_call", output_to_operand_aliasing={{3}: (8, {})} | custom-call | bytes 11439000 | tf_op jit(solution)/shard_map/score/pallas_call | solution.py:431
  34.1 1.9 %collective-permute-start.5 = (f32[5,8,2560]{2,1,0:T(8,128)S(1)}, f32[5,8,2560]{2,1,0:T(8,128)S(1)}, u32[]{:S(2)}, u32[]{:S(2)}) collective-permute-start(f32[5,8,2560]{2,1,0:T(8,128)S(1)} %bitcast.22), channel_id=1, source_target_pairs={{0,16},{1,17},{2,18},{3,19},{4,20},{5,21},{6,22},{7,23},{8,24},{9,... | collective-permute-start | bytes 1228808 | tf_op jit(solution)/shard_map/ppermute | solution.py:362
  35.9 10.8 %all_to_all.5.parts = f32[32,1,128]{2,1,0:T(1,128)S(1)} all-to-all(f32[32,1,128]{2,1,0:T(1,128)S(1)} %get-tuple-element.27), channel_id=1, replica_groups=mesh['ens'=2,'lat'=16] {'ens','lat'}, dimensions={0} | all-to-all | bytes 32768 | tf_op jit(solution)/shard_map/all_to_all | solution.py:448
  46.7 0.0 collective-permute-done.5
  46.7 1.8 %assemble.1 = (f32[5,1,64,640]{3,2,1,0:T(8,128)}, f32[1]{0:T(128)}) custom-call(f32[5,64,384]{2,1,0:T(8,128)S(1)} %get-tuple-element.25.g_own, f32[1,5,8,2560]{3,2,1,0:T(8,128)S(1)} %bitcast.14, f32[32,1,128]{2,1,0:T(1,128)S(1)} %all_to_all.5.parts), custom_call_target="tpu_custom_call" | custom-call | bytes 6642000 | tf_op jit(solution)/shard_map/assemble/pallas_call | solution.py:450
Async XLA Ops:
  0.6 1.1 %copy-start = (f32[5,1,64,640]{3,2,1,0:T(8,128)S(1)}, f32[5,1,64,640]{3,2,1,0:T(8,128)}, u32[]{:S(2)}) copy-start(f32[5,1,64,640]{3,2,1,0:T(8,128)} %members.1) | copy-start | bytes 2457604
  1.8 26.2 %copy-start.3 = (s32[1,5,5]{2,0,1:T(1,128)S(1)}, s32[1,5,5]{2,0,1:T(1,128)}, u32[]{:S(2)}) copy-start(s32[1,5,5]{2,0,1:T(1,128)} %param.10) | copy-start | bytes 304
  2.9 17.9 %collective-permute-start.2 = (f32[5,8,2688]{2,1,0:T(8,128)S(1)}, f32[5,8,2688]{2,1,0:T(8,128)S(1)}, u32[]{:S(2)}, u32[]{:S(2)}) collective-permute-start(f32[5,8,2688]{2,1,0:T(8,128)S(1)} %bitcast.21), channel_id=1, source_target_pairs={{0,16},{1,17},{2,18},{3,19},{4,20},{5,21},{6,22},{7,23},{8,24},{9,... | collective-permute-start | bytes 1290248 | tf_op jit(solution)/shard_map/ppermute | solution.py:362
  6.0 22.0 %collective-permute-start = (f32[4,8,2688]{2,1,0:T(8,128)S(1)}, f32[4,8,2688]{2,1,0:T(8,128)S(1)}, u32[]{:S(2)}, u32[]{:S(2)}) collective-permute-start(f32[4,8,2688]{2,1,0:T(8,128)S(1)} %get-tuple-element.17), channel_id=1, source_target_pairs={{0,1},{1,0},{2,3},{3,2},{4,5},{5,4},{6,7},{7,6},{8,9},{9,8},{10,11... | collective-permute-start | bytes 1032200 | tf_op jit(solution)/shard_map/ppermute | solution.py:372
  6.0 22.0 %collective-permute-start.1 = (f32[4,8,2688]{2,1,0:T(8,128)S(1)}, f32[4,8,2688]{2,1,0:T(8,128)S(1)}, u32[]{:S(2)}, u32[]{:S(2)}) collective-permute-start(f32[4,8,2688]{2,1,0:T(8,128)S(1)} %get-tuple-element.18), channel_id=1, source_target_pairs={{1,2},{2,1},{3,4},{4,3},{5,6},{6,5},{7,8},{8,7},{9,10},{10,9},{11,... | collective-permute-start | bytes 1032200 | tf_op jit(solution)/shard_map/ppermute | solution.py:371
  6.7 24.3 %collective-permute-start.4 = (f32[4,8,2688]{2,1,0:T(8,128)S(1)}, f32[4,8,2688]{2,1,0:T(8,128)S(1)}, u32[]{:S(2)}, u32[]{:S(2)}) collective-permute-start(f32[4,8,2688]{2,1,0:T(8,128)S(1)} %bitcast.23), channel_id=1, source_target_pairs={{1,18},{2,17},{3,20},{4,19},{5,22},{6,21},{7,24},{8,23},{9,26},{10... | collective-permute-start | bytes 1032200 | tf_op jit(solution)/shard_map/ppermute | solution.py:367
  21.5 9.5 %collective-permute-start.3 = (f32[4,8,2688]{2,1,0:T(8,128)S(1)}, f32[4,8,2688]{2,1,0:T(8,128)S(1)}, u32[]{:S(2)}, u32[]{:S(2)}) collective-permute-start(f32[4,8,2688]{2,1,0:T(8,128)S(1)} %bitcast.24), channel_id=1, source_target_pairs={{0,1},{1,0},{2,3},{3,2},{4,5},{5,4},{6,7},{7,6},{8,9},{9,8},{10,11... | collective-permute-start | bytes 1032200 | tf_op jit(solution)/shard_map/ppermute | solution.py:367
  21.6 1.0 %copy-start.1 = (f32[1,64,9,64]{3,1,2,0:T(8,128)S(1)}, f32[1,64,9,64]{3,1,2,0:T(8,128)}, u32[]{:S(2)}) copy-start(f32[1,64,9,64]{3,1,2,0:T(8,128)} %param.12) | copy-start | bytes 442372
  22.5 0.8 %copy-start.2 = (f32[1,5,5,9,5]{3,0,4,2,1:T(1,128)S(1)}, f32[1,5,5,9,5]{3,0,4,2,1:T(1,128)}, u32[]{:S(2)}) copy-start(f32[1,5,5,9,5]{3,0,4,2,1:T(1,128)} %param.11) | copy-start | bytes 13504
  23.4 0.7 %copy-start.4 = (s32[5]{0:T(128)S(1)}, s32[5]{0:T(128)}, u32[]{:S(2)}) copy-start(s32[5]{0:T(128)} %times.1) | copy-start | bytes 64
  27.9 3.0 %copy-start.5 = (f32[80]{0:T(128)S(1)}, f32[80]{0:T(128)}, u32[]{:S(2)}) copy-start(f32[80]{0:T(128)} %constant.2.clone.area) | copy-start | bytes 964
  34.1 12.6 %collective-permute-start.5 = (f32[5,8,2560]{2,1,0:T(8,128)S(1)}, f32[5,8,2560]{2,1,0:T(8,128)S(1)}, u32[]{:S(2)}, u32[]{:S(2)}) collective-permute-start(f32[5,8,2560]{2,1,0:T(8,128)S(1)} %bitcast.22), channel_id=1, source_target_pairs={{0,16},{1,17},{2,18},{3,19},{4,20},{5,21},{6,22},{7,23},{8,24},{9,... | collective-permute-start | bytes 1228808 | tf_op jit(solution)/shard_map/ppermute | solution.py:362

commit v3 on v2

--- a/solution.py
+++ b/solution.py
@@ -200,12 +200,15 @@
     return mixed
 
 
-def own_kernel(sizes, row_taps, weights, own_w, near, far, x_own, split):
+def split_kernel(own_w, split):
+    for r in range(own_w.shape[0]):
+        store_split(split, REACH + r, own_w[r])
+
+
+def own_kernel(sizes, row_taps, weights, own_w, near, far, split_in, x_own, split):
     band, lags, w, reach2, wide = sizes
     kept = w + 2 * reach2
     store_halo(split, near, (), far, (), kept, wide, band)
-    for r in range(band):
-        store_split(split, REACH + r, own_w[r])
     for r in range(band):
         mixed = convolve(row_taps, weights, split, r, lags, band)
         x_own[r] = shift_left(own_w[r], reach2) + gelu(mixed)
@@ -274,32 +277,32 @@
     parts[...] = jnp.broadcast_to(total[None], parts.shape)
 
 
-def assemble_kernel(sizes, g_own, back, parts, out, loss):
+def assemble_kernel(sizes, g_own, back, parts, out, loss, held, sems):
     band, n, w, wide = sizes
     ens = lax.axis_index("ens")
-    groups = g_own.shape[1] // GROUP
-    total = out.shape[3]
-    lane = lax.broadcasted_iota(jnp.int32, (g_own.shape[1], total), 1)
-    span = max(total, wide)
-
-    def one_row(r, _):
-        result = None
-        for step in range(n):
-            if step == 0:
-                cells = g_own[r]
-            else:
-                cells = unpack_rows(back, (step - 1, r), groups, w, wide)
-            cells = jnp.concatenate([cells, jnp.zeros((cells.shape[0], span - wide), cells.dtype)], axis=1)
-            owner = lax.rem(ens + step, n)
-            cells = pltpu.roll(cells, owner * w, axis=1)
-            mine = jnp.logical_and(lane >= owner * w, lane < (owner + 1) * w)
-            result = jnp.where(mine, cells, 0.0) if result is None else jnp.where(mine, cells, result)
-        out[r, 0] = result
-        return 0
-
-    lax.fori_loop(0, band, one_row, 0)
+    c, total = held.shape[1:]
+    lane = lax.broadcasted_iota(jnp.int32, (c, total), 1)
+    copies = [pltpu.make_async_copy(held.at[r], out.at[r, 0], sems.at[r]) for r in range(band)]
+    for p in range(n):
+
+        @pl.when(ens == p)
+        def _():
+            for r in range(band):
+                result = None
+                for owner in range(n):
+                    step = (owner - p) % n
+                    cells = g_own[r] if step == 0 else unpack_rows(back, (step - 1, r), c // GROUP, w, wide)
+                    if wide < total:
+                        cells = jnp.concatenate([cells, jnp.zeros((c, total - wide), cells.dtype)], axis=1)
+                    cells = shift_left(cells, -owner * w)[:, :total]
+                    result = cells if result is None else jnp.where(lane >= owner * w, cells, result)
+                held[r] = result
+                copies[r].start()
+
     cells = band * (parts.shape[0] // n) * total
     loss[0] = jnp.sum(jnp.sum(parts[...], axis=0)[:, :1]) / cells
+    for copy in copies:
+        copy.wait()
 
 
 def shift_pairs(sizes, step):
@@ -372,6 +375,18 @@
     near_own = lax.ppermute(near_own, axes, halo_pairs(sizes, 0, True))
     far_oth = halo_oth(far_oth, False)
 
+    own_shape = jax.ShapeDtypeStruct((ext, 2 * c, wide), jnp.bfloat16)
+    split_own = pl.pallas_call(
+        split_kernel,
+        name="split_own",
+        cost_estimate=takes(2.0),
+        in_specs=[VMEM],
+        out_specs=VMEM,
+        out_shape=own_shape,
+        compiler_params=params(16),
+    )(own_w)
+    filters, mix, target_time, split_own = lax.optimization_barrier((filters, mix, target_time, split_own))
+
     weights, target = pl.pallas_call(
         functools.partial(weights_kernel, (band, n, taps, lags, kinds, w, wide)),
         name="weights",
@@ -398,16 +413,16 @@
 
     split_shape = jax.ShapeDtypeStruct((n - 1, ext, 2 * c, wide), jnp.bfloat16)
 
-    x_own = pl.pallas_call(
+    x_own, _ = pl.pallas_call(
         functools.partial(own_kernel, (band, lags, w, reach2, wide)),
         name="convolve_own",
         cost_estimate=takes(3.0),
-        in_specs=[SMEM] + [VMEM] * 4,
-        out_specs=VMEM,
-        out_shape=jax.ShapeDtypeStruct((band, c, wide), f32),
-        scratch_shapes=[pltpu.VMEM((ext, 2 * c, wide), jnp.bfloat16)],
+        in_specs=[SMEM] + [VMEM] * 5,
+        out_specs=[VMEM] * 2,
+        out_shape=[jax.ShapeDtypeStruct((band, c, wide), f32), own_shape],
+        input_output_aliases={5: 1},
         compiler_params=params(24),
-    )(row_taps, weights, own_w, near_own, far_own)
+    )(row_taps, weights, own_w, near_own, far_own, split_own)
 
     near_oth, states, split_oth = pl.pallas_call(
         functools.partial(receive_kernel, (band, n, w, reach2, wide)),
@@ -452,8 +467,9 @@
         name="assemble",
         cost_estimate=takes(1.8),
         in_specs=[VMEM] * 3,
-        out_specs=[VMEM, SMEM],
+        out_specs=[HBM, SMEM],
         out_shape=[jax.ShapeDtypeStruct(members.shape, f32), jax.ShapeDtypeStruct((1,), f32)],
+        scratch_shapes=[pltpu.VMEM((band, c, total), f32), pltpu.SemaphoreType.DMA((band,))],
         compiler_params=params(16),
     )(g_own, back, parts)
     return (score_grad, loss_value)

time: 48.8 us -> 46.2 us (0.947)
  local copies, waits for them, and re-layouts: 3.59 us -> 1.17 us
    unnamed x12, local copies, waits for them, and re-layouts: 3.59 us -> 1.17 us
  transfers between devices with their start and end apart: 6 -> 6, of which waited for: 1 -> 1; matrix products, arithmetic and copies ran while one was open for 0% -> 0% of each run, Pallas kernels for 15% -> 16%
where the time goes in v3:
time: 46.2 us; the launch traced here: 46 us
  waiting for transfers between devices  13.5 us (29%)
  Pallas kernels  13.4 us (29%)
  blocking collectives  10.8 us (23%)
  starting transfers between devices  6.32 us (14%)
  local copies, waits for them, and re-layouts  1.17 us (3%)
  between operations  0.82 us (2%)
    ppermute x2, waiting for transfers between devices, along_ens(): lax.ppermute(stack[s - 1], axes, shift_pairs(sizes, sign * s))  13.5 us
    all_to_all x1, blocking collectives, per_device(): parts = lax.all_to_all(parts, axes, 0, 0, tiled=True)  10.8 us
    ppermute x2, starting transfers between devices, along_ens(): lax.ppermute(stack[s - 1], axes, shift_pairs(sizes, sign * s))  4.89 us
    pallas_call x1, Pallas kernels, per_device(): pl.pallas_call(functools.partial(weights_kernel, (band, n, taps, lags, ki...  3.91 us
    pallas_call x1, Pallas kernels, per_device(): pl.pallas_call(functools.partial(score_kernel, (band, n, lags, w, reach2,...  3.12 us
    pallas_call x1, Pallas kernels, per_device(): pl.pallas_call(functools.partial(own_kernel, (band, lags, w, reach2, wide...  2.91 us
    pallas_call x1, Pallas kernels, per_device(): pl.pallas_call(functools.partial(assemble_kernel, (band, n, w, wide)), na...  1.65 us
    unnamed x12, local copies, waits for them, and re-layouts  1.17 us
  transfers between devices with their start and end apart: 6, of which 1 were waited for; matrix products, arithmetic and copies ran while one was open for 0% of the time, Pallas kernels for 16%

profile of v3, /device:TPU:0, one launch (start us, length us, event | category | flops | bytes accessed | tf_op | source)
XLA Modules:
  0.0 46.0 jit_solution(12527314629406640939)
XLA Ops:
  0.6 0.0 copy-start
  0.6 1.1 %copy-done = f32[5,1,64,640]{3,2,1,0:T(8,128)S(1)} copy-done((f32[5,1,64,640]{3,2,1,0:T(8,128)S(1)}, f32[5,1,64,640]{3,2,1,0:T(8,128)}, u32[]{:S(2)}) %copy-start) | copy-done | bytes 819224
  1.8 1.2 %prepare.1 = (f32[5,64,384]{2,1,0:T(8,128)S(1)}, f32[4,8,2688]{2,1,0:T(8,128)S(1)}, f32[4,8,2688]{2,1,0:T(8,128)S(1)}, f32[1,5,8,2688]{3,2,1,0:T(8,128)S(1)}, f32[1,4,8,2688]{3,2,1,0:T(8,128)S(1)}) custom-call(f32[5,1,64,640]{3,2,1,0:T(8,128)S(1)} %copy-done), custom_call_target="tpu_custom_call" | custom-call | bytes 4428000 | tf_op jit(solution)/shard_map/prepare/pallas_call | solution.py:347
  2.9 0.0 copy-start.1
  3.0 0.0 copy-start.2
  3.0 0.0 copy-start.4
  3.0 3.0 %collective-permute-start.2 = (f32[5,8,2688]{2,1,0:T(8,128)S(1)}, f32[5,8,2688]{2,1,0:T(8,128)S(1)}, u32[]{:S(2)}, u32[]{:S(2)}) collective-permute-start(f32[5,8,2688]{2,1,0:T(8,128)S(1)} %bitcast.21), channel_id=1, source_target_pairs={{0,16},{1,17},{2,18},{3,19},{4,20},{5,21},{6,22},{7,23},{8,24},{9,... | collective-permute-start | bytes 1290248 | tf_op jit(solution)/shard_map/ppermute | solution.py:365
  6.0 0.0 collective-permute-start
  6.0 0.7 %collective-permute-start.1 = (f32[4,8,2688]{2,1,0:T(8,128)S(1)}, f32[4,8,2688]{2,1,0:T(8,128)S(1)}, u32[]{:S(2)}, u32[]{:S(2)}) collective-permute-start(f32[4,8,2688]{2,1,0:T(8,128)S(1)} %get-tuple-element.26), channel_id=1, source_target_pairs={{1,2},{2,1},{3,4},{4,3},{5,6},{6,5},{7,8},{8,7},{9,10},{10,9},{11,... | collective-permute-start | bytes 1032200 | tf_op jit(solution)/shard_map/ppermute | solution.py:374
  6.7 0.7 %collective-permute-start.4 = (f32[4,8,2688]{2,1,0:T(8,128)S(1)}, f32[4,8,2688]{2,1,0:T(8,128)S(1)}, u32[]{:S(2)}, u32[]{:S(2)}) collective-permute-start(f32[4,8,2688]{2,1,0:T(8,128)S(1)} %bitcast.23), channel_id=1, source_target_pairs={{1,18},{2,17},{3,20},{4,19},{5,22},{6,21},{7,24},{8,23},{9,26},{10... | collective-permute-start | bytes 1032200 | tf_op jit(solution)/shard_map/ppermute | solution.py:370
  7.4 13.5 %collective-permute-done.2 = f32[5,8,2688]{2,1,0:T(8,128)S(1)} collective-permute-done((f32[5,8,2688]{2,1,0:T(8,128)S(1)}, f32[5,8,2688]{2,1,0:T(8,128)S(1)}, u32[]{:S(2)}, u32[]{:S(2)}) %collective-permute-start.2) | collective-permute-done | bytes 430112 | tf_op jit(solution)/shard_map/ppermute | solution.py:365
  20.9 0.6 %receive.1 = (f32[1,4,8,2688]{3,2,1,0:T(8,128)S(1)}, f32[1,5,64,384]{3,2,1,0:T(8,128)S(1)}, bf16[1,13,128,384]{3,2,1,0:T(8,128)(2,1)S(1)}) custom-call(f32[1,5,8,2688]{3,2,1,0:T(8,128)S(1)} %bitcast.13), custom_call_target="tpu_custom_call" | custom-call | bytes 2214000 | tf_op jit(solution)/shard_map/receive/pallas_call | solution.py:427
  21.5 0.1 collective-permute-start.3
  21.6 0.1 split_own.1.split_in
  21.7 0.0 copy-done.1
  21.7 0.0 copy-done.2
  21.7 0.0 copy-done.4
  21.7 0.0 copy-start.3
  21.7 3.9 %weights.1 = (bf16[5,320,1024]{2,1,0:T(8,128)(2,1)S(1)}, f32[5,64,384]{2,1,0:T(8,128)S(1)}) custom-call(s32[5]{0:T(128)S(1)} %copy-done.4, f32[5,5,5,1,9]{4,3,2,1,0:T(1,128)S(1)} %bitcast.18, f32[9,64,64]{2,1,0:T(8,128)S(1)} %bitcast.17, f32[4,5,64,640]{3,2,1,0:T(8,128)} %truth.1), custom_call_target="tpu_custom_call" | custom-call | bytes 14760000 | tf_op jit(solution)/shard_map/weights/pallas_call | solution.py:390
  25.6 0.0 collective-permute-done.near
  25.6 0.0 collective-permute-done.1.far
  25.6 0.0 copy-done.3
  25.7 0.0 copy-start.5
  25.7 2.9 %convolve_own.1 = (f32[5,64,384]{2,1,0:T(8,128)S(1)}, bf16[13,128,384]{2,1,0:T(8,128)(2,1)S(1)}) custom-call(s32[5,1,5]{2,1,0:T(1,128)S(1)} %bitcast.19, bf16[5,320,1024]{2,1,0:T(8,128)(2,1)S(1)} %get-tuple-element.24.weights, f32[5,64,384]{2,1,0:T(8,128)S(1)} %get-tuple-element.20.own_w, ...), custom_call_target="tpu_custom_call", output_to_operand_aliasing={{1}: (5, {})} | custom-call | bytes 11070000 | tf_op jit(solution)/shard_map/convolve_own/pallas_call | solution.py:416
  28.6 0.0 collective-permute-done.4
  28.6 0.0 collective-permute-done.3
  28.6 0.0 copy-done.5
  28.6 3.1 %score.1 = (f32[5,64,384]{2,1,0:T(8,128)S(1)}, f32[1,5,8,2560]{3,2,1,0:T(8,128)S(1)}, f32[32,1,128]{2,1,0:T(1,128)S(1)}, bf16[1,13,128,384]{3,2,1,0:T(8,128)(2,1)S(1)}) custom-call(s32[5,1,5]{2,1,0:T(1,128)S(1)} %bitcast.20, f32[80]{0:T(128)S(1)} %copy-done.5, bf16[5,320,1024]{2,1,0:T(8,128)(2,1)S(1)} %get-tuple-element.24.weights, ...), custom_call_target="tpu_custom_call", output_to_operand_aliasing={{3}: (8, {})} | custom-call | bytes 11439000 | tf_op jit(solution)/shard_map/score/pallas_call | solution.py:446
  31.7 1.8 %collective-permute-start.5 = (f32[5,8,2560]{2,1,0:T(8,128)S(1)}, f32[5,8,2560]{2,1,0:T(8,128)S(1)}, u32[]{:S(2)}, u32[]{:S(2)}) collective-permute-start(f32[5,8,2560]{2,1,0:T(8,128)S(1)} %bitcast.22), channel_id=1, source_target_pairs={{0,16},{1,17},{2,18},{3,19},{4,20},{5,21},{6,22},{7,23},{8,24},{9,... | collective-permute-start | bytes 1228808 | tf_op jit(solution)/shard_map/ppermute | solution.py:365
  33.6 10.8 %all_to_all.5.parts = f32[32,1,128]{2,1,0:T(1,128)S(1)} all-to-all(f32[32,1,128]{2,1,0:T(1,128)S(1)} %get-tuple-element.37), channel_id=1, replica_groups=mesh['ens'=2,'lat'=16] {'ens','lat'}, dimensions={0} | all-to-all | bytes 32768 | tf_op jit(solution)/shard_map/all_to_all | solution.py:463
  44.4 0.0 collective-permute-done.5
  44.4 1.7 %assemble.1 = (f32[5,1,64,640]{3,2,1,0:T(8,128)}, f32[1]{0:T(128)}) custom-call(f32[5,64,384]{2,1,0:T(8,128)S(1)} %get-tuple-element.35.g_own, f32[1,5,8,2560]{3,2,1,0:T(8,128)S(1)} %bitcast.14, f32[32,1,128]{2,1,0:T(1,128)S(1)} %all_to_all.5.parts), custom_call_target="tpu_custom_call" | custom-call | bytes 6642000 | tf_op jit(solution)/shard_map/assemble/pallas_call | solution.py:465
Async XLA Ops:
  0.6 1.1 %copy-start = (f32[5,1,64,640]{3,2,1,0:T(8,128)S(1)}, f32[5,1,64,640]{3,2,1,0:T(8,128)}, u32[]{:S(2)}) copy-start(f32[5,1,64,640]{3,2,1,0:T(8,128)} %members.1) | copy-start | bytes 2457604
  2.9 18.7 %copy-start.1 = (f32[1,64,9,64]{3,1,2,0:T(8,128)S(1)}, f32[1,64,9,64]{3,1,2,0:T(8,128)}, u32[]{:S(2)}) copy-start(f32[1,64,9,64]{3,1,2,0:T(8,128)} %param.12) | copy-start | bytes 442372
  3.0 18.7 %copy-start.2 = (f32[1,5,5,9,5]{3,0,4,2,1:T(1,128)S(1)}, f32[1,5,5,9,5]{3,0,4,2,1:T(1,128)}, u32[]{:S(2)}) copy-start(f32[1,5,5,9,5]{3,0,4,2,1:T(1,128)} %param.11) | copy-start | bytes 13504
  3.0 18.7 %copy-start.4 = (s32[5]{0:T(128)S(1)}, s32[5]{0:T(128)}, u32[]{:S(2)}) copy-start(s32[5]{0:T(128)} %times) | copy-start | bytes 64
  3.0 17.9 %collective-permute-start.2 = (f32[5,8,2688]{2,1,0:T(8,128)S(1)}, f32[5,8,2688]{2,1,0:T(8,128)S(1)}, u32[]{:S(2)}, u32[]{:S(2)}) collective-permute-start(f32[5,8,2688]{2,1,0:T(8,128)S(1)} %bitcast.21), channel_id=1, source_target_pairs={{0,16},{1,17},{2,18},{3,19},{4,20},{5,21},{6,22},{7,23},{8,24},{9,... | collective-permute-start | bytes 1290248 | tf_op jit(solution)/shard_map/ppermute | solution.py:365
  6.0 19.6 %collective-permute-start = (f32[4,8,2688]{2,1,0:T(8,128)S(1)}, f32[4,8,2688]{2,1,0:T(8,128)S(1)}, u32[]{:S(2)}, u32[]{:S(2)}) collective-permute-start(f32[4,8,2688]{2,1,0:T(8,128)S(1)} %get-tuple-element.25), channel_id=1, source_target_pairs={{0,1},{1,0},{2,3},{3,2},{4,5},{5,4},{6,7},{7,6},{8,9},{9,8},{10,11... | collective-permute-start | bytes 1032200 | tf_op jit(solution)/shard_map/ppermute | solution.py:375
  6.0 19.6 %collective-permute-start.1 = (f32[4,8,2688]{2,1,0:T(8,128)S(1)}, f32[4,8,2688]{2,1,0:T(8,128)S(1)}, u32[]{:S(2)}, u32[]{:S(2)}) collective-permute-start(f32[4,8,2688]{2,1,0:T(8,128)S(1)} %get-tuple-element.26), channel_id=1, source_target_pairs={{1,2},{2,1},{3,4},{4,3},{5,6},{6,5},{7,8},{8,7},{9,10},{10,9},{11,... | collective-permute-start | bytes 1032200 | tf_op jit(solution)/shard_map/ppermute | solution.py:374
  6.7 21.9 %collective-permute-start.4 = (f32[4,8,2688]{2,1,0:T(8,128)S(1)}, f32[4,8,2688]{2,1,0:T(8,128)S(1)}, u32[]{:S(2)}, u32[]{:S(2)}) collective-permute-start(f32[4,8,2688]{2,1,0:T(8,128)S(1)} %bitcast.23), channel_id=1, source_target_pairs={{1,18},{2,17},{3,20},{4,19},{5,22},{6,21},{7,24},{8,23},{9,26},{10... | collective-permute-start | bytes 1032200 | tf_op jit(solution)/shard_map/ppermute | solution.py:370
  21.5 7.1 %collective-permute-start.3 = (f32[4,8,2688]{2,1,0:T(8,128)S(1)}, f32[4,8,2688]{2,1,0:T(8,128)S(1)}, u32[]{:S(2)}, u32[]{:S(2)}) collective-permute-start(f32[4,8,2688]{2,1,0:T(8,128)S(1)} %bitcast.24), channel_id=1, source_target_pairs={{0,1},{1,0},{2,3},{3,2},{4,5},{5,4},{6,7},{7,6},{8,9},{9,8},{10,11... | collective-permute-start | bytes 1032200 | tf_op jit(solution)/shard_map/ppermute | solution.py:370
  21.7 4.0 %copy-start.3 = (s32[1,5,5]{2,0,1:T(1,128)S(1)}, s32[1,5,5]{2,0,1:T(1,128)}, u32[]{:S(2)}) copy-start(s32[1,5,5]{2,0,1:T(1,128)} %param.10) | copy-start | bytes 304
  25.7 3.0 %copy-start.5 = (f32[80]{0:T(128)S(1)}, f32[80]{0:T(128)}, u32[]{:S(2)}) copy-start(f32[80]{0:T(128)} %constant.2.clone.area) | copy-start | bytes 964
  31.7 12.6 %collective-permute-start.5 = (f32[5,8,2560]{2,1,0:T(8,128)S(1)}, f32[5,8,2560]{2,1,0:T(8,128)S(1)}, u32[]{:S(2)}, u32[]{:S(2)}) collective-permute-start(f32[5,8,2560]{2,1,0:T(8,128)S(1)} %bitcast.22), channel_id=1, source_target_pairs={{0,16},{1,17},{2,18},{3,19},{4,20},{5,21},{6,22},{7,23},{8,24},{9,... | collective-permute-start | bytes 1228808 | tf_op jit(solution)/shard_map/ppermute | solution.py:365
